TPU v7x, 32 devices: a whole 2x2x4 slice. The times are simulated.
32 devices in a mesh: event: 2 (over x), phi: 16 (over z, y, core).
Axes of the slice: x: 2, y: 2, z: 4, core: 2. Of those that a mesh axis runs over, the one named last changes fastest.
Arguments:
- hit_feats: bfloat16 [12, 131072], P(None, ('event', 'phi')), parts along dimension 1, may hold values from -6 to 6
- layer_ids: int32 [131072], P(('event', 'phi')), parts along dimension 0, may hold values from 0 to 15
- edge_tiles: bfloat16 [1024, 8, 128, 128], P(('event', 'phi')), parts along dimension 0
- src_blocks: int32 [1024, 8], P(('event', 'phi')), parts along dimension 0, may hold values from 0 to 159
- live_slots: int32 [1024], P(('event', 'phi')), parts along dimension 0, may hold values from 1 to 8, as said below
- anchor_hits: int32 [32768], P(('event', 'phi')), parts along dimension 0, may hold values from 0 to 4095
- positive_hits: int32 [32768], P(('event', 'phi')), parts along dimension 0, may hold values from 0 to 20479
- negative_hits: int32 [32768], P(('event', 'phi')), parts along dimension 0, may hold values from 0 to 20479
- w_enc: bfloat16 [12, 128], replicated, may hold values from -1.75 to 1.75
- layer_table: bfloat16 [16, 128], replicated, may hold values from -3 to 3
- w_self: bfloat16 [2, 128, 128], replicated, may hold values from -0.5 to 0.5
- w_agg: bfloat16 [2, 128, 128], replicated, may hold values from -0.5 to 0.5
- w_out: bfloat16 [2, 128, 128], replicated, may hold values from -0.5 to 0.5
Outputs:
- loss: float32 [2], P('event'), parts along dimension 0
- grad_enc: float32 [24, 128], P('event'), parts along dimension 0
- grad_table: float32 [32, 128], P('event'), parts along dimension 0
- grad_self: float32 [4, 128, 128], P('event'), parts along dimension 0
- grad_agg: float32 [4, 128, 128], P('event'), parts along dimension 0
- grad_out: float32 [4, 128, 128], P('event'), parts along dimension 0
There are 2 independent parts, one for each index of `event`. A program takes and returns all parts, laid end to end along the dimension named above; an argument that names none is the same for every part. Nothing has to cross between parts.
Inputs may be any that keep to these rules, and one draw needn't show every extreme that they name: `live_slots`: in every draw some node block has all 8 slots live.
All inputs are finite; a program needn't handle non-finite values.
Results may differ from a plain program's by a relative error of at most 0.0022.
Values may be sent and summed in bfloat16 or wider, within the bound.
A program may use at most 128 MiB of HBM per device.

v0:
```python
import math

import jax
import jax.numpy as jnp
from jax import lax
from jax.sharding import PartitionSpec as P

loss_divisor = 64.0


def shifted(value, axis, steps):
    count = lax.axis_size(axis)
    pairs = [(source, (source + steps) % count) for source in range(count)]
    return lax.ppermute(value, axis, pairs)


def contract_rows(left_side, right_side):
    return lax.dot_general(
        left_side, right_side, (((0,), (0,)), ((), ())), preferred_element_type=jnp.float32
    )


def contract_cols(left_side, right_side):
    return lax.dot_general(
        left_side, right_side, (((1,), (1,)), ((), ())), preferred_element_type=jnp.float32
    )


def contract_inner(left_side, right_side):
    return lax.dot_general(
        left_side, right_side, (((1,), (0,)), ((), ())), preferred_element_type=jnp.float32
    )


def contrast_terms(window, anchor_here, positive_here, negative_here, centre, latent_width):
    anchor = window[centre + anchor_here].astype(jnp.float32)
    positive = window[positive_here].astype(jnp.float32)
    negative = window[negative_here].astype(jnp.float32)
    inv_root = 1.0 / math.sqrt(latent_width)
    score_gap = (jnp.sum(anchor * negative, axis=1) - jnp.sum(anchor * positive, axis=1)) * inv_root
    return (score_gap, anchor, positive, negative)


def contrast_grad(
    score_gap,
    anchor,
    positive,
    negative,
    anchor_here,
    positive_here,
    negative_here,
    centre,
    window_shape,
    latent_width,
):
    weight_coef = (jax.nn.sigmoid(score_gap) * (1.0 / (loss_divisor * math.sqrt(latent_width))))[
        :, None
    ]
    gradient = jnp.zeros(window_shape, jnp.float32)
    gradient = gradient.at[centre + anchor_here].add(weight_coef * (negative - positive))
    gradient = gradient.at[positive_here].add(-weight_coef * anchor)
    gradient = gradient.at[negative_here].add(weight_coef * anchor)
    return gradient


def neighbour_window(latents):
    ahead_near = shifted(latents, "phi", -1)
    ahead_far = shifted(latents, "phi", -2)
    behind_near = shifted(latents, "phi", 1)
    behind_far = shifted(latents, "phi", 2)
    return jnp.concatenate([behind_far, behind_near, latents, ahead_near, ahead_far], axis=0)


def return_window(window_grad, hit_count):
    pieces = window_grad.reshape(5, hit_count, window_grad.shape[1])
    lower_far = pieces[0].astype(jnp.bfloat16)
    lower_near = pieces[1].astype(jnp.bfloat16)
    upper_near = pieces[3].astype(jnp.bfloat16)
    upper_far = pieces[4].astype(jnp.bfloat16)
    below_far = shifted(upper_far, "phi", 2)
    below_near = shifted(upper_near, "phi", 1)
    above_near = shifted(lower_near, "phi", -1)
    above_far = shifted(lower_far, "phi", -2)
    received = below_far.astype(jnp.float32) + below_near.astype(jnp.float32)
    received = received + above_near.astype(jnp.float32) + above_far.astype(jnp.float32)
    return pieces[2] + received


def block_product(edge_tiles, src_blocks, live_mask, window):
    block_rows = edge_tiles.shape[2]
    latent_width = window.shape[1]
    blocks = window.reshape(-1, block_rows, latent_width)
    chosen = jnp.where(live_mask[:, :, None, None], blocks[src_blocks], jnp.zeros((), blocks.dtype))
    return jnp.einsum("bsij,bsjw->biw", edge_tiles, chosen, preferred_element_type=jnp.float32)


def block_transpose(edge_tiles, src_blocks, live_mask, agg_grad):
    block_count, slot_count, block_rows = (
        edge_tiles.shape[0],
        edge_tiles.shape[1],
        edge_tiles.shape[2],
    )
    latent_width = agg_grad.shape[2]
    contrib = jnp.einsum("bsij,biw->bsjw", edge_tiles, agg_grad, preferred_element_type=jnp.float32)
    contrib = jnp.where(live_mask[:, :, None, None], contrib, 0.0)
    return jax.ops.segment_sum(
        contrib.reshape(block_count * slot_count, block_rows, latent_width),
        src_blocks.reshape(block_count * slot_count),
        num_segments=5 * block_count,
    )


def body(
    hit_feats,
    layer_ids,
    edge_tiles,
    src_blocks,
    live_slots,
    anchor_hits,
    positive_hits,
    negative_hits,
    w_enc,
    layer_table,
    w_self,
    w_agg,
    w_out,
):
    block_count, slot_count, block_rows = (
        edge_tiles.shape[0],
        edge_tiles.shape[1],
        edge_tiles.shape[2],
    )
    latent_width = w_enc.shape[1]
    hit_count = block_count * block_rows
    layer_total = w_self.shape[0]
    live_mask = jnp.arange(slot_count, dtype=jnp.int32)[None, :] < live_slots[:, None]
    onehot = (
        jnp.arange(layer_table.shape[0], dtype=jnp.int32)[:, None] == layer_ids[None, :]
    ).astype(jnp.bfloat16)
    encoded = contract_rows(hit_feats, w_enc) + contract_rows(onehot, layer_table)
    squashed = jnp.tanh(encoded)
    latents = squashed.astype(jnp.bfloat16)
    stored = []
    for layer_index in range(layer_total):
        window = neighbour_window(latents)
        aggregated = (
            block_product(edge_tiles, src_blocks, live_mask, window)
            .reshape(hit_count, latent_width)
            .astype(jnp.bfloat16)
        )
        activation = jnp.dot(
            latents, w_self[layer_index], preferred_element_type=jnp.float32
        ) + jnp.dot(aggregated, w_agg[layer_index], preferred_element_type=jnp.float32)
        hidden = jax.nn.relu(activation).astype(jnp.bfloat16)
        updated = (
            latents.astype(jnp.float32)
            + jnp.dot(hidden, w_out[layer_index], preferred_element_type=jnp.float32)
        ).astype(jnp.bfloat16)
        stored.append((latents, aggregated, activation, hidden))
        latents = updated
    window = neighbour_window(latents)
    centre = 2 * hit_count
    score_gap, anchor, positive, negative = contrast_terms(
        window, anchor_hits, positive_hits, negative_hits, centre, latent_width
    )
    loss_part = jnp.sum(jax.nn.softplus(score_gap))
    window_grad = contrast_grad(
        score_gap,
        anchor,
        positive,
        negative,
        anchor_hits,
        positive_hits,
        negative_hits,
        centre,
        window.shape,
        latent_width,
    )
    gradient = return_window(window_grad, hit_count)
    self_grads = [None] * layer_total
    agg_grads = [None] * layer_total
    out_grads = [None] * layer_total
    for layer_index in range(layer_total - 1, -1, -1):
        before, aggregated, activation, hidden = stored[layer_index]
        upstream = gradient.astype(jnp.bfloat16)
        out_grads[layer_index] = contract_rows(hidden, upstream)
        hidden_grad = contract_cols(upstream, w_out[layer_index])
        act_grad = jnp.where(activation > 0, hidden_grad, 0.0).astype(jnp.bfloat16)
        self_grads[layer_index] = contract_rows(before, act_grad)
        agg_grads[layer_index] = contract_rows(aggregated, act_grad)
        agg_grad = contract_cols(act_grad, w_agg[layer_index]).astype(jnp.bfloat16)
        direct = gradient + contract_cols(act_grad, w_self[layer_index])
        spread = block_transpose(
            edge_tiles,
            src_blocks,
            live_mask,
            agg_grad.reshape(block_count, block_rows, latent_width),
        )
        gradient = direct + return_window(spread.reshape(5 * hit_count, latent_width), hit_count)
    encoded_grad = (gradient * (1.0 - squashed * squashed)).astype(jnp.bfloat16)
    grad_enc = contract_inner(hit_feats, encoded_grad)
    grad_table = contract_inner(onehot, encoded_grad)
    summed = lax.psum(
        (
            grad_enc,
            grad_table,
            jnp.stack(self_grads),
            jnp.stack(agg_grads),
            jnp.stack(out_grads),
            loss_part,
        ),
        "phi",
    )
    triplet_total = anchor_hits.shape[0] * lax.axis_size("phi")
    loss = (summed[5] / triplet_total).reshape(1)
    return (loss, summed[0], summed[1], summed[2], summed[3], summed[4])


def solution(mesh):
    in_specs = (
        P(None, ("event", "phi")),
        P(("event", "phi")),
        P(("event", "phi"), None, None, None),
        P(("event", "phi"), None),
        P(("event", "phi")),
        P(("event", "phi")),
        P(("event", "phi")),
        P(("event", "phi")),
        P(),
        P(),
        P(),
        P(),
        P(),
    )
    out_specs = (
        P("event"),
        P("event", None),
        P("event", None),
        P("event", None, None),
        P("event", None, None),
        P("event", None, None),
    )
    return jax.shard_map(body, mesh=mesh, in_specs=in_specs, out_specs=out_specs, check_vma=False)
```

profile of v0, /device:TPU:0, one launch (start us, length us, event | category | flops | bytes accessed | tf_op | source)
XLA Modules:
  0.0 817.9 jit_solution(6428048118215018878)
XLA Ops:
  8.1 1.2 fusion.77
  9.2 2.8 fusion.76
  12.1 3.0 collective-permute-start
  15.1 4.4 collective-permute-start.2
  20.1 1.7 fusion.51
  21.9 50.5 %collective-permute-done = bf16[4096,128]{1,0:T(8,128)(2,1)} collective-permute-done((bf16[4096,128]{1,0:T(8,128)(2,1)S(1)}, bf16[4096,128]{1,0:T(8,128)(2,1)}, u32[]{:S(2)}, u32[]{:S(2)}) %collective-permute-start) | collective-permute-done | bytes 1048608 | tf_op jit(solution)/shard_map/ppermute | solution.py:14
  72.3 2.3 constant_dynamic-update-slice_fusion.4
  74.6 2.3 constant_dynamic-update-slice_fusion.3
  79.0 7.2 collective-permute-done.3
  87.2 11.2 %gather_fusion = bf16[256,128,128]{2,1,0:T(8,128)(2,1)} fusion(bf16[160,128,128]{2,1,0:T(8,128)(2,1)} %bitcast.1, s32[1024]{0:T(1024)S(1)} %pad_clamp_fusion), kind=kCustom, calls=%fused_computation | custom fusion | bytes 16778240 | tf_op jit(solution)/shard_map/gather | solution.py:93
  98.4 8.3 %bitcast_convert_fusion.1 = bf16[32,128,128]{1,2,0:T(8,128)(2,1)S(1)} fusion(bf16[32,8,128,128]{3,2,1,0:T(8,128)(2,1)} %param.15, bf16[32,8,128,128]{3,2,1,0:T(8,128)(2,1)} %bitcast.122, pred[32,8]{1,0:T(8,128)(4,1)S(1)} %iota_compare_fusion.3), kind=kOutput, calls=%fused_computation.46 | convolution fusion | flops 1078460416 | bytes 17826048 | tf_op jit(solution)/shard_map/bsij,bsjw->biw/dot_general | solution.py:94
  108.1 3.3 collective-permute-start.4
  111.4 4.4 collective-permute-start.6
  116.4 1.7 fusion.44
  118.2 50.5 %collective-permute-done.4 = bf16[4096,128]{1,0:T(8,128)(2,1)S(1)} collective-permute-done((bf16[4096,128]{1,0:T(8,128)(2,1)S(1)}, bf16[4096,128]{1,0:T(8,128)(2,1)S(1)}, u32[]{:S(2)}, u32[]{:S(2)}) %collective-permute-start.4) | collective-permute-done | bytes 1048608 | tf_op jit(solution)/shard_map/ppermute | solution.py:14
  172.9 8.7 %collective-permute-done.7 = bf16[4096,128]{1,0:T(8,128)(2,1)S(1)} collective-permute-done((bf16[4096,128]{1,0:T(8,128)(2,1)S(1)}, bf16[4096,128]{1,0:T(8,128)(2,1)S(1)}, u32[]{:S(2)}, u32[]{:S(2)}) %collective-permute-start.7) | collective-permute-done | bytes 1048608 | tf_op jit(solution)/shard_map/ppermute | solution.py:14
  182.6 11.2 %gather_fusion.1 = bf16[256,128,128]{2,1,0:T(8,128)(2,1)} fusion(bf16[160,128,128]{2,1,0:T(8,128)(2,1)} %bitcast.10, s32[1024]{0:T(1024)S(1)} %pad_clamp_fusion), kind=kCustom, calls=%fused_computation.1 | custom fusion | bytes 16778240 | tf_op jit(solution)/shard_map/gather | solution.py:93
  193.8 8.3 %bitcast_convert_fusion = bf16[32,128,128]{1,2,0:T(8,128)(2,1)S(1)} fusion(bf16[32,8,128,128]{3,2,1,0:T(8,128)(2,1)} %param.15, bf16[32,8,128,128]{3,2,1,0:T(8,128)(2,1)} %bitcast.121, pred[32,8]{1,0:T(8,128)(4,1)S(1)} %iota_compare_fusion.3), kind=kOutput, calls=%fused_computation.45 | convolution fusion | flops 1078460416 | bytes 17826048 | tf_op jit(solution)/shard_map/bsij,bsjw->biw/dot_general | solution.py:94
  202.6 1.1 copy-done.12
  205.1 4.5 collective-permute-start.10
  209.6 1.5 collective-permute-start.11
  211.1 51.2 %collective-permute-done.8 = bf16[4096,128]{1,0:T(8,128)(2,1)S(1)} collective-permute-done((bf16[4096,128]{1,0:T(8,128)(2,1)S(1)}, bf16[4096,128]{1,0:T(8,128)(2,1)S(1)}, u32[]{:S(2)}, u32[]{:S(2)}) %collective-permute-start.8) | collective-permute-done | bytes 1048608 | tf_op jit(solution)/shard_map/ppermute | solution.py:14
  266.5 8.9 %collective-permute-done.11 = bf16[4096,128]{1,0:T(8,128)(2,1)S(1)} collective-permute-done((bf16[4096,128]{1,0:T(8,128)(2,1)S(1)}, bf16[4096,128]{1,0:T(8,128)(2,1)S(1)}, u32[]{:S(2)}, u32[]{:S(2)}) %collective-permute-start.11) | collective-permute-done | bytes 1048608 | tf_op jit(solution)/shard_map/ppermute | solution.py:14
  276.5 6.0 gather_fusion.3
  282.5 6.0 gather_fusion.4
  288.6 6.0 gather_fusion.2
  295.6 11.2 %scatter_custom_fusion = f32[20480,128]{1,0:T(8,128)} fusion(s32[1024]{0:T(1024)S(1)} %get-tuple-element.33, f32[]{:T(128)} %constant.14.clone.1, bf16[1024,128]{1,0:T(8,128)(2,1)S(1)} %gather_fusion.4, bf16[1024,128]{1,0:T(8,128)(2,1)S(1)} %gather_fusion.3, f32[1024]{0:T(1024)S(1)} %get-tuple-element.15), kind=kCustom, calls=%fused_computation.18 | custom fusion | flops 655360 | bytes 11014148 | tf_op jit(solution)/shard_map/scatter-add | solution.py:60
  306.8 13.9 %scatter_custom_fusion.1 = f32[20480,128]{1,0:T(8,128)} fusion(f32[20480,128]{1,0:T(8,128)} %scatter_custom_fusion, s32[1024]{0:T(1024)S(1)} %get-tuple-element.31, bf16[1024,128]{1,0:T(8,128)(2,1)S(1)} %gather_fusion.2, f32[1024]{0:T(1024)S(1)} %get-tuple-element.14), kind=kCustom, calls=%fused_computation.64 | custom fusion | flops 393216 | bytes 10752000 | tf_op jit(solution)/shard_map/scatter-add | solution.py:61
  320.7 13.9 %scatter_custom_fusion.2 = f32[20480,128]{1,0:T(8,128)} fusion(f32[20480,128]{1,0:T(8,128)} %scatter_custom_fusion.1, s32[1024]{0:T(1024)S(1)} %get-tuple-element.38, bf16[1024,128]{1,0:T(8,128)(2,1)S(1)} %gather_fusion.2, f32[1024]{0:T(1024)S(1)} %get-tuple-element.15), kind=kCustom, calls=%fused_computation.65 | custom fusion | flops 393216 | bytes 10752000 | tf_op jit(solution)/shard_map/scatter-add | solution.py:62
  334.6 4.6 convert.18
  339.2 2.1 fusion.75
  342.5 4.4 collective-permute-start.14
  346.9 1.3 collective-permute-start.15
  348.4 51.2 %collective-permute-done.12 = bf16[4096,128]{1,0:T(8,128)(2,1)S(1)} collective-permute-done((bf16[4096,128]{1,0:T(8,128)(2,1)}, bf16[4096,128]{1,0:T(8,128)(2,1)S(1)}, u32[]{:S(2)}, u32[]{:S(2)}) %collective-permute-start.12) | collective-permute-done | bytes 1048608 | tf_op jit(solution)/shard_map/ppermute | solution.py:14
  399.6 13.1 %collective-permute-done.15 = bf16[4096,128]{1,0:T(8,128)(2,1)} collective-permute-done((bf16[4096,128]{1,0:T(8,128)(2,1)}, bf16[4096,128]{1,0:T(8,128)(2,1)}, u32[]{:S(2)}, u32[]{:S(2)}) %collective-permute-start.15) | collective-permute-done | bytes 1048608 | tf_op jit(solution)/shard_map/ppermute | solution.py:14
  412.6 3.0 slice_add_fusion
  417.5 11.7 %convolution_select_fusion.1 = f32[32,128,8,128]{3,1,2,0:T(8,128)} fusion(bf16[32,128,128,1]{2,1,3,0:T(8,128)(2,1)S(1)} %bitcast.124, bf16[32,8,128,128]{3,2,1,0:T(8,128)(2,1)} %param.15, pred[32,8]{1,0:T(8,128)(4,1)S(1)} %iota_compare_fusion.3), kind=kOutput, calls=%fused_computation.11 | convolution fusion | flops 1077936128 | bytes 26214656 | tf_op jit(solution)/shard_map/bsij,biw->bsjw/dot_general | solution.py:104
  429.2 17.4 %copy.26 = f32[256,128,128]{2,1,0:T(8,128)} copy(f32[256,128,128]{1,2,0:T(8,128)} %bitcast.118) | data formatting | bytes 33554432 | tf_op jit(solution)/shard_map/reshape | solution.py:107
  446.6 5.3 broadcast.77.clone
  452.0 52.5 %scatter_fusion = f32[160,128,128]{2,1,0:T(8,128)} fusion(f32[160,128,128]{2,1,0:T(8,128)} %broadcast.77.clone, s32[256]{0:T(256)S(1)} %reshape.190, f32[256,128,128]{2,1,0:T(8,128)} %copy.26), kind=kCustom, calls=%fused_computation.8 | custom fusion | flops 4194304 | bytes 50332672 | tf_op jit(solution)/shard_map/scatter-add | solution.py:106
  504.4 5.3 convert.19
  510.2 4.4 collective-permute-start.18
  514.6 2.1 collective-permute-start.19
  516.8 1.8 slice.132
  518.6 1.1 convolution_bitcast_fusion.2
  520.2 47.2 %collective-permute-done.16 = bf16[4096,128]{1,0:T(8,128)(2,1)S(1)} collective-permute-done((bf16[4096,128]{1,0:T(8,128)(2,1)S(1)}, bf16[4096,128]{1,0:T(8,128)(2,1)S(1)}, u32[]{:S(2)}, u32[]{:S(2)}) %collective-permute-start.16) | collective-permute-done | bytes 1048608 | tf_op jit(solution)/shard_map/ppermute | solution.py:14
  567.4 10.6 %collective-permute-done.19 = bf16[4096,128]{1,0:T(8,128)(2,1)S(1)} collective-permute-done((bf16[4096,128]{1,0:T(8,128)(2,1)S(1)}, bf16[4096,128]{1,0:T(8,128)(2,1)S(1)}, u32[]{:S(2)}, u32[]{:S(2)}) %collective-permute-start.19) | collective-permute-done | bytes 1048608 | tf_op jit(solution)/shard_map/ppermute | solution.py:14
  580.6 2.1 slice-done.1
  582.8 7.1 convolution_select_fusion
  589.9 17.4 %copy.28 = f32[256,128,128]{2,1,0:T(8,128)} copy(f32[256,128,128]{1,2,0:T(8,128)} %bitcast.117) | data formatting | bytes 33554432 | tf_op jit(solution)/shard_map/reshape | solution.py:107
  607.3 5.3 broadcast.77
  612.7 52.5 %scatter_fusion.1 = f32[160,128,128]{2,1,0:T(8,128)} fusion(f32[160,128,128]{2,1,0:T(8,128)} %broadcast.77, s32[256]{0:T(256)S(1)} %reshape.190, f32[256,128,128]{2,1,0:T(8,128)} %copy.28), kind=kCustom, calls=%fused_computation.9 | custom fusion | flops 4194304 | bytes 50332672 | tf_op jit(solution)/shard_map/scatter-add | solution.py:106
  665.1 5.3 convert.20
  670.4 2.1 fusion.73
  672.5 4.4 collective-permute-start.22
  677.0 2.0 collective-permute-start.23
  679.5 3.3 slice.137
  686.3 44.8 %collective-permute-done.20 = bf16[4096,128]{1,0:T(8,128)(2,1)} collective-permute-done((bf16[4096,128]{1,0:T(8,128)(2,1)}, bf16[4096,128]{1,0:T(8,128)(2,1)}, u32[]{:S(2)}, u32[]{:S(2)}) %collective-permute-start.20) | collective-permute-done | bytes 1048608 | tf_op jit(solution)/shard_map/ppermute | solution.py:14
  731.1 11.0 %collective-permute-done.23 = bf16[4096,128]{1,0:T(8,128)(2,1)} collective-permute-done((bf16[4096,128]{1,0:T(8,128)(2,1)}, bf16[4096,128]{1,0:T(8,128)(2,1)}, u32[]{:S(2)}, u32[]{:S(2)}) %collective-permute-start.23) | collective-permute-done | bytes 1048608 | tf_op jit(solution)/shard_map/ppermute | solution.py:14
  742.1 3.4 bitcast_add_fusion
  746.6 57.7 %all-reduce = (f32[]{:T(128)}, f32[12,128]{1,0:T(8,128)}, f32[16,128]{1,0:T(8,128)}) all-reduce(f32[]{:T(128)} %get-tuple-element.28, f32[12,128]{1,0:T(8,128)S(1)} %convolution_bitcast_fusion.6, f32[16,128]{1,0:T(8,128)S(1)} %fusion.36), channel_id=1, replica_groups=mesh['event'=2,'phi'=16] {'phi'}, use_global_device_ids=true, to_apply=%region_3.4 | all-reduce | flops 3585 | bytes 28680 | tf_op jit(solution)/shard_map/psum | solution.py:203
  805.0 1.6 copy.57
  806.6 1.6 copy.58
  808.1 1.6 copy.59
  (144 shorter events, 31.6 us)
Async XLA Ops:
  7.2 0.9 copy-start
  7.2 12.7 %copy-start.29 = (s32[32,8]{0,1:T(8,128)S(1)}, s32[32,8]{0,1:T(8,128)}, u32[]{:S(2)}) copy-start(s32[32,8]{0,1:T(8,128)} %param.16) | copy-start | bytes 3076
  7.2 12.8 %copy-start.33 = (s32[32]{0:T(128)S(1)}, s32[32]{0:T(128)}, u32[]{:S(2)}) copy-start(s32[32]{0:T(128)} %param.17) | copy-start | bytes 388
  7.2 12.9 %copy-start.26 = (bf16[2,128,128]{2,1,0:T(8,128)(2,1)S(1)}, bf16[2,128,128]{2,1,0:T(8,128)(2,1)}, u32[]{:S(2)}) copy-start(bf16[2,128,128]{2,1,0:T(8,128)(2,1)} %param.23) | copy-start | bytes 196612
  7.2 797.8 %all-reduce.4.cloned.1.call-start = ((), (), s32[]{:S(2)}) async-start(), calls=%async_computation | async-start | bytes 786432 | tf_op jit(solution)/shard_map/psum | solution.py:203
  12.1 95.1 %copy-start.9 = (bf16[4096,128]{1,0:T(8,128)(2,1)}, bf16[4096,128]{1,0:T(8,128)(2,1)S(1)}, u32[]{:S(2)}) copy-start(bf16[4096,128]{1,0:T(8,128)(2,1)S(1)} %get-tuple-element.35) | copy-start | bytes 3145732
  12.1 60.3 %collective-permute-start = (bf16[4096,128]{1,0:T(8,128)(2,1)S(1)}, bf16[4096,128]{1,0:T(8,128)(2,1)}, u32[]{:S(2)}, u32[]{:S(2)}) collective-permute-start(bf16[4096,128]{1,0:T(8,128)(2,1)S(1)} %get-tuple-element.35), channel_id=1, source_target_pairs={{0,2},{1,3},{2,4},{3,5},{4,6},{5,7},{6,8},{7,9},{8,10},{9,11},{10,... | collective-permute-start | bytes 3145736 | tf_op jit(solution)/shard_map/ppermute | solution.py:14
  15.0 59.5 %collective-permute-start.1 = (bf16[4096,128]{1,0:T(8,128)(2,1)S(1)}, bf16[4096,128]{1,0:T(8,128)(2,1)}, u32[]{:S(2)}, u32[]{:S(2)}) collective-permute-start(bf16[4096,128]{1,0:T(8,128)(2,1)S(1)} %get-tuple-element.35), channel_id=1, source_target_pairs={{0,1},{1,2},{2,3},{3,4},{4,5},{5,6},{6,7},{7,8},{8,9},{9,10},{10,1... | collective-permute-start | bytes 3145736 | tf_op jit(solution)/shard_map/ppermute | solution.py:14
  15.1 62.8 %collective-permute-start.2 = (bf16[4096,128]{1,0:T(8,128)(2,1)S(1)}, bf16[4096,128]{1,0:T(8,128)(2,1)S(1)}, u32[]{:S(2)}, u32[]{:S(2)}) collective-permute-start(bf16[4096,128]{1,0:T(8,128)(2,1)S(1)} %get-tuple-element.35), channel_id=1, source_target_pairs={{0,15},{1,0},{2,1},{3,2},{4,3},{5,4},{6,5},{7,6},{8,7},{9,8},{10,9... | collective-permute-start | bytes 3145736 | tf_op jit(solution)/shard_map/ppermute | solution.py:14
  19.5 66.7 %collective-permute-start.3 = (bf16[4096,128]{1,0:T(8,128)(2,1)S(1)}, bf16[4096,128]{1,0:T(8,128)(2,1)S(1)}, u32[]{:S(2)}, u32[]{:S(2)}) collective-permute-start(bf16[4096,128]{1,0:T(8,128)(2,1)S(1)} %get-tuple-element.35), channel_id=1, source_target_pairs={{0,14},{1,15},{2,0},{3,1},{4,2},{5,3},{6,4},{7,5},{8,6},{9,7},{10,... | collective-permute-start | bytes 3145736 | tf_op jit(solution)/shard_map/ppermute | solution.py:14
  98.4 8.4 %copy-start.18 = (f32[4096,128]{1,0:T(8,128)S(1)}, f32[4096,128]{1,0:T(8,128)}, u32[]{:S(2)}) copy-start(f32[4096,128]{1,0:T(8,128)} %fusion.51) | copy-start | bytes 6291460
  98.4 8.4 %copy-start.25 = (bf16[2,128,128]{2,1,0:T(8,128)(2,1)S(1)}, bf16[2,128,128]{2,1,0:T(8,128)(2,1)}, u32[]{:S(2)}) copy-start(bf16[2,128,128]{2,1,0:T(8,128)(2,1)} %param.24) | copy-start | bytes 196612
  106.7 11.4 %copy-start.20 = (bf16[32,128,128]{1,2,0:T(8,128)(2,1)}, bf16[32,128,128]{1,2,0:T(8,128)(2,1)S(1)}, u32[]{:S(2)}) copy-start(bf16[32,128,128]{1,2,0:T(8,128)(2,1)S(1)} %bitcast_convert_fusion.1) | copy-start | bytes 3145732
  106.7 0.9 copy-start.24
  108.1 64.8 %copy-start.11 = (bf16[4096,128]{1,0:T(8,128)(2,1)}, bf16[4096,128]{1,0:T(8,128)(2,1)S(1)}, u32[]{:S(2)}) copy-start(bf16[4096,128]{1,0:T(8,128)(2,1)S(1)} %fusion.12) | copy-start | bytes 3145732
  108.1 60.5 %collective-permute-start.4 = (bf16[4096,128]{1,0:T(8,128)(2,1)S(1)}, bf16[4096,128]{1,0:T(8,128)(2,1)S(1)}, u32[]{:S(2)}, u32[]{:S(2)}) collective-permute-start(bf16[4096,128]{1,0:T(8,128)(2,1)S(1)} %fusion.12), channel_id=1, source_target_pairs={{0,2},{1,3},{2,4},{3,5},{4,6},{5,7},{6,8},{7,9},{8,10},{9,11},{10,... | collective-permute-start | bytes 3145736 | tf_op jit(solution)/shard_map/ppermute | solution.py:14
  111.4 58.3 %collective-permute-start.5 = (bf16[4096,128]{1,0:T(8,128)(2,1)S(1)}, bf16[4096,128]{1,0:T(8,128)(2,1)S(1)}, u32[]{:S(2)}, u32[]{:S(2)}) collective-permute-start(bf16[4096,128]{1,0:T(8,128)(2,1)S(1)} %fusion.12), channel_id=1, source_target_pairs={{0,1},{1,2},{2,3},{3,4},{4,5},{5,6},{6,7},{7,8},{8,9},{9,10},{10,1... | collective-permute-start | bytes 3145736 | tf_op jit(solution)/shard_map/ppermute | solution.py:14
  111.4 60.4 %collective-permute-start.6 = (bf16[4096,128]{1,0:T(8,128)(2,1)S(1)}, bf16[4096,128]{1,0:T(8,128)(2,1)S(1)}, u32[]{:S(2)}, u32[]{:S(2)}) collective-permute-start(bf16[4096,128]{1,0:T(8,128)(2,1)S(1)} %fusion.12), channel_id=1, source_target_pairs={{0,15},{1,0},{2,1},{3,2},{4,3},{5,4},{6,5},{7,6},{8,7},{9,8},{10,9... | collective-permute-start | bytes 3145736 | tf_op jit(solution)/shard_map/ppermute | solution.py:14
  115.8 65.8 %collective-permute-start.7 = (bf16[4096,128]{1,0:T(8,128)(2,1)S(1)}, bf16[4096,128]{1,0:T(8,128)(2,1)S(1)}, u32[]{:S(2)}, u32[]{:S(2)}) collective-permute-start(bf16[4096,128]{1,0:T(8,128)(2,1)S(1)} %fusion.12), channel_id=1, source_target_pairs={{0,14},{1,15},{2,0},{3,1},{4,2},{5,3},{6,4},{7,5},{8,6},{9,7},{10,... | collective-permute-start | bytes 3145736 | tf_op jit(solution)/shard_map/ppermute | solution.py:14
  193.8 8.4 %copy-start.17 = (f32[4096,128]{1,0:T(8,128)S(1)}, f32[4096,128]{1,0:T(8,128)}, u32[]{:S(2)}) copy-start(f32[4096,128]{1,0:T(8,128)} %fusion.44) | copy-start | bytes 6291460
  202.2 61.2 %copy-start.22 = (bf16[32,128,128]{1,2,0:T(8,128)(2,1)}, bf16[32,128,128]{1,2,0:T(8,128)(2,1)S(1)}, u32[]{:S(2)}) copy-start(bf16[32,128,128]{1,2,0:T(8,128)(2,1)S(1)} %bitcast_convert_fusion) | copy-start | bytes 3145732
  202.2 1.6 copy-start.12
  202.2 2.9 copy-start.30
  202.2 2.9 copy-start.31
  202.2 2.9 copy-start.32
  203.8 61.7 %copy-start.1 = (f32[4096,128]{1,0:T(8,128)}, f32[4096,128]{1,0:T(8,128)S(1)}, u32[]{:S(2)}) copy-start(f32[4096,128]{1,0:T(8,128)S(1)} %convolution_add_fusion.3) | copy-start | bytes 6291460
  204.2 58.1 %collective-permute-start.8 = (bf16[4096,128]{1,0:T(8,128)(2,1)S(1)}, bf16[4096,128]{1,0:T(8,128)(2,1)S(1)}, u32[]{:S(2)}, u32[]{:S(2)}) collective-permute-start(bf16[4096,128]{1,0:T(8,128)(2,1)S(1)} %fusion.13), channel_id=1, source_target_pairs={{0,2},{1,3},{2,4},{3,5},{4,6},{5,7},{6,8},{7,9},{8,10},{9,11},{10,... | collective-permute-start | bytes 3145736 | tf_op jit(solution)/shard_map/ppermute | solution.py:14
  205.0 58.3 %collective-permute-start.9 = (bf16[4096,128]{1,0:T(8,128)(2,1)S(1)}, bf16[4096,128]{1,0:T(8,128)(2,1)S(1)}, u32[]{:S(2)}, u32[]{:S(2)}) collective-permute-start(bf16[4096,128]{1,0:T(8,128)(2,1)S(1)} %fusion.13), channel_id=1, source_target_pairs={{0,1},{1,2},{2,3},{3,4},{4,5},{5,6},{6,7},{7,8},{8,9},{9,10},{10,1... | collective-permute-start | bytes 3145736 | tf_op jit(solution)/shard_map/ppermute | solution.py:14
  205.1 60.4 %collective-permute-start.10 = (bf16[4096,128]{1,0:T(8,128)(2,1)S(1)}, bf16[4096,128]{1,0:T(8,128)(2,1)S(1)}, u32[]{:S(2)}, u32[]{:S(2)}) collective-permute-start(bf16[4096,128]{1,0:T(8,128)(2,1)S(1)} %fusion.13), channel_id=1, source_target_pairs={{0,15},{1,0},{2,1},{3,2},{4,3},{5,4},{6,5},{7,6},{8,7},{9,8},{10,9... | collective-permute-start | bytes 3145736 | tf_op jit(solution)/shard_map/ppermute | solution.py:14
  209.6 65.8 %collective-permute-start.11 = (bf16[4096,128]{1,0:T(8,128)(2,1)S(1)}, bf16[4096,128]{1,0:T(8,128)(2,1)S(1)}, u32[]{:S(2)}, u32[]{:S(2)}) collective-permute-start(bf16[4096,128]{1,0:T(8,128)(2,1)S(1)} %fusion.13), channel_id=1, source_target_pairs={{0,14},{1,15},{2,0},{3,1},{4,2},{5,3},{6,4},{7,5},{8,6},{9,7},{10,... | collective-permute-start | bytes 3145736 | tf_op jit(solution)/shard_map/ppermute | solution.py:14
  341.3 58.3 %collective-permute-start.12 = (bf16[4096,128]{1,0:T(8,128)(2,1)}, bf16[4096,128]{1,0:T(8,128)(2,1)S(1)}, u32[]{:S(2)}, u32[]{:S(2)}) collective-permute-start(bf16[4096,128]{1,0:T(8,128)(2,1)} %get-tuple-element.24), channel_id=1, source_target_pairs={{0,2},{1,3},{2,4},{3,5},{4,6},{5,7},{6,8},{7,9},{8,10},{9,11},{10,... | collective-permute-start | bytes 3145736 | tf_op jit(solution)/shard_map/ppermute | solution.py:14
  342.0 57.6 %collective-permute-start.13 = (bf16[4096,128]{1,0:T(8,128)(2,1)}, bf16[4096,128]{1,0:T(8,128)(2,1)}, u32[]{:S(2)}, u32[]{:S(2)}) collective-permute-start(bf16[4096,128]{1,0:T(8,128)(2,1)} %get-tuple-element.27), channel_id=1, source_target_pairs={{0,1},{1,2},{2,3},{3,4},{4,5},{5,6},{6,7},{7,8},{8,9},{9,10},{10,1... | collective-permute-start | bytes 3145736 | tf_op jit(solution)/shard_map/ppermute | solution.py:14
  342.5 57.1 %collective-permute-start.14 = (bf16[4096,128]{1,0:T(8,128)(2,1)}, bf16[4096,128]{1,0:T(8,128)(2,1)}, u32[]{:S(2)}, u32[]{:S(2)}) collective-permute-start(bf16[4096,128]{1,0:T(8,128)(2,1)} %get-tuple-element.26), channel_id=1, source_target_pairs={{0,15},{1,0},{2,1},{3,2},{4,3},{5,4},{6,5},{7,6},{8,7},{9,8},{10,9... | collective-permute-start | bytes 3145736 | tf_op jit(solution)/shard_map/ppermute | solution.py:14
  346.9 65.7 %collective-permute-start.15 = (bf16[4096,128]{1,0:T(8,128)(2,1)}, bf16[4096,128]{1,0:T(8,128)(2,1)}, u32[]{:S(2)}, u32[]{:S(2)}) collective-permute-start(bf16[4096,128]{1,0:T(8,128)(2,1)} %get-tuple-element.25), channel_id=1, source_target_pairs={{0,14},{1,15},{2,0},{3,1},{4,2},{5,3},{6,4},{7,5},{8,6},{9,7},{10,... | collective-permute-start | bytes 3145736 | tf_op jit(solution)/shard_map/ppermute | solution.py:14
  348.4 67.3 %copy-start.2 = (f32[4096,128]{1,0:T(8,128)S(1)}, f32[4096,128]{1,0:T(8,128)}, u32[]{:S(2)}) copy-start(f32[4096,128]{1,0:T(8,128)} %copy-done.1) | copy-start | bytes 6291460
  415.7 1.3 copy-start.7
  509.7 8.9 %copy-start.23 = (bf16[32,128,128]{1,2,0:T(8,128)(2,1)S(1)}, bf16[32,128,128]{1,2,0:T(8,128)(2,1)}, u32[]{:S(2)}) copy-start(bf16[32,128,128]{1,2,0:T(8,128)(2,1)} %copy-done.22) | copy-start | bytes 3145732
  510.1 9.6 %copy-start.3 = (f32[4096,128]{1,0:T(8,128)S(1)}, f32[4096,128]{1,0:T(8,128)}, u32[]{:S(2)}) copy-start(f32[4096,128]{1,0:T(8,128)} %copy-done.1) | copy-start | bytes 6291460
  510.1 9.6 %copy-start.8 = (f32[4096,128]{1,0:T(8,128)S(1)}, f32[4096,128]{1,0:T(8,128)}, u32[]{:S(2)}) copy-start(f32[4096,128]{1,0:T(8,128)} %copy-done.7) | copy-start | bytes 6291460
  510.1 57.3 %collective-permute-start.16 = (bf16[4096,128]{1,0:T(8,128)(2,1)S(1)}, bf16[4096,128]{1,0:T(8,128)(2,1)S(1)}, u32[]{:S(2)}, u32[]{:S(2)}) collective-permute-start(bf16[4096,128]{1,0:T(8,128)(2,1)S(1)} %bitcast.132), channel_id=1, source_target_pairs={{0,2},{1,3},{2,4},{3,5},{4,6},{5,7},{6,8},{7,9},{8,10},{9,11},{10,... | collective-permute-start | bytes 3145736 | tf_op jit(solution)/shard_map/ppermute | solution.py:14
  510.2 57.3 %collective-permute-start.17 = (bf16[4096,128]{1,0:T(8,128)(2,1)S(1)}, bf16[4096,128]{1,0:T(8,128)(2,1)S(1)}, u32[]{:S(2)}, u32[]{:S(2)}) collective-permute-start(bf16[4096,128]{1,0:T(8,128)(2,1)S(1)} %bitcast.131), channel_id=1, source_target_pairs={{0,1},{1,2},{2,3},{3,4},{4,5},{5,6},{6,7},{7,8},{8,9},{9,10},{10,1... | collective-permute-start | bytes 3145736 | tf_op jit(solution)/shard_map/ppermute | solution.py:14
  510.2 57.2 %collective-permute-start.18 = (bf16[4096,128]{1,0:T(8,128)(2,1)S(1)}, bf16[4096,128]{1,0:T(8,128)(2,1)S(1)}, u32[]{:S(2)}, u32[]{:S(2)}) collective-permute-start(bf16[4096,128]{1,0:T(8,128)(2,1)S(1)} %bitcast.130), channel_id=1, source_target_pairs={{0,15},{1,0},{2,1},{3,2},{4,3},{5,4},{6,5},{7,6},{8,7},{9,8},{10,9... | collective-permute-start | bytes 3145736 | tf_op jit(solution)/shard_map/ppermute | solution.py:14
  514.6 63.4 %collective-permute-start.19 = (bf16[4096,128]{1,0:T(8,128)(2,1)S(1)}, bf16[4096,128]{1,0:T(8,128)(2,1)S(1)}, u32[]{:S(2)}, u32[]{:S(2)}) collective-permute-start(bf16[4096,128]{1,0:T(8,128)(2,1)S(1)} %bitcast.129), channel_id=1, source_target_pairs={{0,14},{1,15},{2,0},{3,1},{4,2},{5,3},{6,4},{7,5},{8,6},{9,7},{10,... | collective-permute-start | bytes 3145736 | tf_op jit(solution)/shard_map/ppermute | solution.py:14
  578.0 2.6 slice-start
  578.6 4.2 slice-start.1
  579.1 10.8 %copy-start.4 = (f32[4096,128]{1,0:T(8,128)}, f32[4096,128]{1,0:T(8,128)S(1)}, u32[]{:S(2)}) copy-start(f32[4096,128]{1,0:T(8,128)S(1)} %fusion.10) | copy-start | bytes 6291460
  579.6 10.3 %copy-start.14 = (bf16[4096,128]{1,0:T(8,128)(2,1)}, bf16[4096,128]{1,0:T(8,128)(2,1)S(1)}, u32[]{:S(2)}) copy-start(bf16[4096,128]{1,0:T(8,128)(2,1)S(1)} %fusion.16) | copy-start | bytes 3145732
  670.4 8.6 %copy-start.13 = (bf16[4096,128]{1,0:T(8,128)(2,1)S(1)}, bf16[4096,128]{1,0:T(8,128)(2,1)}, u32[]{:S(2)}) copy-start(bf16[4096,128]{1,0:T(8,128)(2,1)} %copy-done.11) | copy-start | bytes 3145732
  672.5 10.3 %copy-start.5 = (f32[4096,128]{1,0:T(8,128)S(1)}, f32[4096,128]{1,0:T(8,128)}, u32[]{:S(2)}) copy-start(f32[4096,128]{1,0:T(8,128)} %copy-done.4) | copy-start | bytes 6291460
  672.5 58.6 %collective-permute-start.20 = (bf16[4096,128]{1,0:T(8,128)(2,1)}, bf16[4096,128]{1,0:T(8,128)(2,1)}, u32[]{:S(2)}, u32[]{:S(2)}) collective-permute-start(bf16[4096,128]{1,0:T(8,128)(2,1)} %bitcast.33), channel_id=1, source_target_pairs={{0,2},{1,3},{2,4},{3,5},{4,6},{5,7},{6,8},{7,9},{8,10},{9,11},{10,... | collective-permute-start | bytes 3145736 | tf_op jit(solution)/shard_map/ppermute | solution.py:14
  672.5 58.6 %collective-permute-start.21 = (bf16[4096,128]{1,0:T(8,128)(2,1)}, bf16[4096,128]{1,0:T(8,128)(2,1)}, u32[]{:S(2)}, u32[]{:S(2)}) collective-permute-start(bf16[4096,128]{1,0:T(8,128)(2,1)} %bitcast.34), channel_id=1, source_target_pairs={{0,1},{1,2},{2,3},{3,4},{4,5},{5,6},{6,7},{7,8},{8,9},{9,10},{10,1... | collective-permute-start | bytes 3145736 | tf_op jit(solution)/shard_map/ppermute | solution.py:14
  672.5 58.6 %collective-permute-start.22 = (bf16[4096,128]{1,0:T(8,128)(2,1)}, bf16[4096,128]{1,0:T(8,128)(2,1)}, u32[]{:S(2)}, u32[]{:S(2)}) collective-permute-start(bf16[4096,128]{1,0:T(8,128)(2,1)} %bitcast.35), channel_id=1, source_target_pairs={{0,15},{1,0},{2,1},{3,2},{4,3},{5,4},{6,5},{7,6},{8,7},{9,8},{10,9... | collective-permute-start | bytes 3145736 | tf_op jit(solution)/shard_map/ppermute | solution.py:14
  676.9 7.0 copy-start.15
  676.9 7.0 copy-start.21
  677.0 65.1 %collective-permute-start.23 = (bf16[4096,128]{1,0:T(8,128)(2,1)}, bf16[4096,128]{1,0:T(8,128)(2,1)}, u32[]{:S(2)}, u32[]{:S(2)}) collective-permute-start(bf16[4096,128]{1,0:T(8,128)(2,1)} %bitcast.36), channel_id=1, source_target_pairs={{0,14},{1,15},{2,0},{3,1},{4,2},{5,3},{6,4},{7,5},{8,6},{9,7},{10,... | collective-permute-start | bytes 3145736 | tf_op jit(solution)/shard_map/ppermute | solution.py:14
  679.5 5.0 copy-start.27
  679.5 5.7 copy-start.10
  685.1 60.3 %copy-start.6 = (f32[4096,128]{1,0:T(8,128)S(1)}, f32[4096,128]{1,0:T(8,128)}, u32[]{:S(2)}) copy-start(f32[4096,128]{1,0:T(8,128)} %copy-done.4) | copy-start | bytes 6291460
  685.2 60.3 %copy-start.16 = (bf16[4096,128]{1,0:T(8,128)(2,1)S(1)}, bf16[4096,128]{1,0:T(8,128)(2,1)}, u32[]{:S(2)}) copy-start(bf16[4096,128]{1,0:T(8,128)(2,1)} %copy-done.14) | copy-start | bytes 3145732
  686.3 59.2 %copy-start.19 = (f32[4096,128]{1,0:T(8,128)S(1)}, f32[4096,128]{1,0:T(8,128)}, u32[]{:S(2)}) copy-start(f32[4096,128]{1,0:T(8,128)} %get-tuple-element.36) | copy-start | bytes 6291460
  745.5 0.9 copy-start.28
Sparse Core Ops, SparseCore 0:
  686.4 107.5 all-reduce.3
where the time goes:
time: 827 us; the launch traced here: 818 us
  waiting for transfers between devices  355 us (43%)
  other arithmetic  169 us (20%)
  local copies, waits for them, and re-layouts  125 us (15%)
  blocking collectives  57.7 us (7%)
  matrix products  51.6 us (6%)
  starting transfers between devices  43 us (5%)
  between operations  16.6 us (2%)
    ppermute x24, waiting for transfers between devices, shifted(): return lax.ppermute(value, axis, pairs)  355 us
    scatter-add x2, other arithmetic, block_transpose(): jax.ops.segment_sum(contrib.reshape(block_count * slot_count, block_rows,...  105 us
    psum x1, blocking collectives, body(): lax.psum((grad_enc, grad_table, jnp.stack(self_grads), jnp.stack(agg_grad...  57.7 us
    ppermute x24, starting transfers between devices, shifted(): return lax.ppermute(value, axis, pairs)  43 us
    reshape x2, local copies, waits for them, and re-layouts, block_transpose(): contrib.reshape(block_count * slot_count, block_rows, latent_width)  34.9 us
    unnamed x88, local copies, waits for them, and re-layouts  26 us
    gather x2, local copies, waits for them, and re-layouts, block_product(): blocks[src_blocks]  22.3 us
    dot_general x2, matrix products, block_transpose(): jnp.einsum('bsij,biw->bsjw', edge_tiles, agg_grad, preferred_element_type...  18.9 us
  transfers between devices with their start and end apart: 25, of which 12 were waited for; matrix products, arithmetic and copies ran while one was open for 4% of the time, Pallas kernels for 0%

commit v1 on v0

v1 whole, which is shorter than its diff:
```python
import functools
import math

import jax
import jax.numpy as jnp
from jax import lax
from jax.experimental import pallas as pl
from jax.experimental.pallas import tpu as pltpu
from jax.sharding import PartitionSpec as P

loss_divisor = 64.0
F32 = jnp.float32
BF16 = jnp.bfloat16
VMEM_BYTES = 60 * 1024 * 1024


def dot(left, right, left_dim, right_dim):
    return lax.dot_general(
        left, right, (((left_dim,), (right_dim,)), ((), ())), preferred_element_type=F32
    )


def full(shape):
    return pl.BlockSpec(shape, lambda *_: (0,) * len(shape))


def params():
    return pltpu.CompilerParams(
        dimension_semantics=("arbitrary",), vmem_limit_bytes=VMEM_BYTES
    )


def permute_far(value, steps):
    count = lax.axis_size("phi")
    return lax.ppermute(value, "phi", [(s, (s + steps) % count) for s in range(count)])


def permute_sibling(value):
    count = lax.axis_size("phi")
    return lax.ppermute(value, "phi", [(s, s ^ 1) for s in range(count)])


def permute_cross(value):
    count = lax.axis_size("phi")
    return lax.ppermute(
        value, "phi", [(s, (s + (1 if s % 2 else -1)) % count) for s in range(count)]
    )


def window_pieces(latents, is_even):
    below = permute_far(latents, 2)
    above = permute_far(latents, -2)
    sibling = permute_sibling(latents)
    cross = permute_sibling(jnp.where(is_even, above, below))
    return below, latents, above, sibling, cross


def return_pieces(below, above, sibling, cross, is_even):
    cross_in = permute_sibling(cross).astype(F32)
    sibling_in = permute_sibling(sibling)
    zero = jnp.zeros((), F32)
    above_out = (above + jnp.where(is_even, cross_in, zero)).astype(BF16)
    below_out = (below + jnp.where(is_even, zero, cross_in)).astype(BF16)
    from_below = permute_far(above_out, 2)
    from_above = permute_far(below_out, -2)
    return from_below, from_above, sibling_in


def aggregate_group(index_ref, tiles_ref, window_ref, step, group, slots, rows, zero_ok=None):
    results = []
    for g in range(group):
        tile = jnp.concatenate([tiles_ref[g, s] for s in range(slots)], axis=1)
        source = jnp.concatenate(
            [
                window_ref[
                    pl.ds(
                        pl.multiple_of(index_ref[(step * group + g) * slots + s] * rows, rows),
                        rows,
                    ),
                    :,
                ]
                for s in range(slots)
            ],
            axis=0,
        )
        results.append(dot(tile, source, 1, 0).astype(BF16))
    return jnp.concatenate(results, axis=0)


def node_update(own, aggregated, w_self, w_agg, w_out):
    activation = dot(own, w_self, 1, 0) + dot(aggregated, w_agg, 1, 0)
    hidden = jnp.maximum(activation, 0.0).astype(BF16)
    updated = (own.astype(F32) + dot(hidden, w_out, 1, 0)).astype(BF16)
    return hidden, updated


def first_forward(
    group,
    index_ref,
    tiles_ref,
    feats_ref,
    wcat_ref,
    w_self_ref,
    w_agg_ref,
    w_out_ref,
    before_ref,
    agg_ref,
    hidden_ref,
    updated_ref,
    window_ref,
):
    step = pl.program_id(0)
    slots, rows = tiles_ref.shape[1], tiles_ref.shape[2]
    span = group * rows
    total = feats_ref.shape[1]

    @pl.when(step == 0)
    def _():
        def encode(i, carry):
            at = pl.multiple_of(i * 512, 512)
            encoded = dot(feats_ref[:, pl.ds(at, 512)], wcat_ref[...], 0, 0)
            window_ref[pl.ds(at, 512), :] = jnp.tanh(encoded).astype(BF16)
            return carry

        lax.fori_loop(0, total // 512, encode, 0)
        window_ref[pl.ds(total, rows), :] = jnp.zeros((rows, window_ref.shape[1]), BF16)

    aggregated = aggregate_group(index_ref, tiles_ref, window_ref, step, group, slots, rows)
    own = window_ref[pl.ds(pl.multiple_of(total // 5 + step * span, span), span), :]
    hidden, updated = node_update(own, aggregated, w_self_ref[...], w_agg_ref[...], w_out_ref[...])
    before_ref[...] = own
    agg_ref[...] = aggregated
    hidden_ref[...] = hidden
    updated_ref[...] = updated


def later_forward(
    group,
    index_ref,
    tiles_ref,
    below_ref,
    own_ref,
    above_ref,
    sibling_ref,
    cross_ref,
    w_self_ref,
    w_agg_ref,
    w_out_ref,
    agg_ref,
    hidden_ref,
    updated_ref,
    window_ref,
    sems,
):
    step = pl.program_id(0)
    slots, rows = tiles_ref.shape[1], tiles_ref.shape[2]
    span = group * rows
    hits = own_ref.shape[0]

    @pl.when(step == 0)
    def _():
        copies = [
            pltpu.make_async_copy(piece, window_ref.at[pl.ds(k * hits, hits)], sems.at[k])
            for k, piece in enumerate((below_ref, own_ref, above_ref, sibling_ref, cross_ref))
        ]
        for copy in copies:
            copy.start()
        window_ref[pl.ds(5 * hits, rows), :] = jnp.zeros((rows, window_ref.shape[1]), BF16)
        for copy in copies:
            copy.wait()

    aggregated = aggregate_group(index_ref, tiles_ref, window_ref, step, group, slots, rows)
    own = window_ref[pl.ds(pl.multiple_of(hits + step * span, span), span), :]
    hidden, updated = node_update(own, aggregated, w_self_ref[...], w_agg_ref[...], w_out_ref[...])
    agg_ref[...] = aggregated
    hidden_ref[...] = hidden
    updated_ref[...] = updated


def contrast_kernel(
    inv_root,
    anchor_ref,
    positive_ref,
    negative_ref,
    below_ref,
    own_ref,
    above_ref,
    sibling_ref,
    cross_ref,
    loss_ref,
    gbelow_ref,
    gown_ref,
    gabove_ref,
    gsibling_ref,
    gcross_ref,
    window_ref,
    grad_pos_ref,
    grad_neg_ref,
    grad_anchor_ref,
    a_ref,
    p_ref,
    n_ref,
):
    hits = own_ref.shape[0]
    count = a_ref.shape[0]
    width = own_ref.shape[1]
    for k, piece in enumerate((below_ref, own_ref, above_ref, sibling_ref, cross_ref)):

        def widen(i, carry, k=k, piece=piece):
            at = pl.multiple_of(i * 256, 256)
            window_ref[pl.ds(k * hits + at, 256), :] = piece[pl.ds(at, 256), :].astype(F32)
            zeros = jnp.zeros((256, width), F32)
            grad_pos_ref[pl.ds(k * hits + at, 256), :] = zeros
            grad_neg_ref[pl.ds(k * hits + at, 256), :] = zeros
            if k == 0:
                grad_anchor_ref[pl.ds(at, 256), :] = zeros
            return carry

        lax.fori_loop(0, hits // 256, widen, 0)

    def fetch(i, carry):
        at = pl.multiple_of(i * 8, 8)
        for index_ref, offset, target in (
            (anchor_ref, hits, a_ref),
            (positive_ref, 0, p_ref),
            (negative_ref, 0, n_ref),
        ):
            target[pl.ds(at, 8), :] = jnp.concatenate(
                [window_ref[pl.ds(index_ref[i * 8 + u] + offset, 1), :] for u in range(8)], axis=0
            )
        return carry

    lax.fori_loop(0, count // 8, fetch, 0)

    def score(i, total):
        at = pl.multiple_of(i * 128, 128)
        anchor = a_ref[pl.ds(at, 128), :]
        positive = p_ref[pl.ds(at, 128), :]
        negative = n_ref[pl.ds(at, 128), :]
        gap = (
            jnp.sum(anchor * negative, axis=1, keepdims=True)
            - jnp.sum(anchor * positive, axis=1, keepdims=True)
        ) * inv_root
        soft = jnp.maximum(gap, 0.0) + jnp.log1p(jnp.exp(-jnp.abs(gap)))
        coef = jax.nn.sigmoid(gap) * (inv_root / loss_divisor)
        p_ref[pl.ds(at, 128), :] = coef * (negative - positive)
        a_ref[pl.ds(at, 128), :] = coef * anchor
        return total + jnp.sum(soft, axis=0, keepdims=True)

    total = lax.fori_loop(0, count // 128, score, jnp.zeros((1, 1), F32))
    loss_ref[...] = jnp.broadcast_to(total, loss_ref.shape)

    def spread(i, carry):
        for u in range(8):
            t = i * 8 + u
            moved = a_ref[pl.ds(t, 1), :]
            here = pl.ds(anchor_ref[t], 1)
            grad_anchor_ref[here, :] = grad_anchor_ref[here, :] + p_ref[pl.ds(t, 1), :]
            there = pl.ds(positive_ref[t], 1)
            grad_pos_ref[there, :] = grad_pos_ref[there, :] - moved
            away = pl.ds(negative_ref[t], 1)
            grad_neg_ref[away, :] = grad_neg_ref[away, :] + moved
        return carry

    lax.fori_loop(0, count // 8, spread, 0)

    for k, target in enumerate((gbelow_ref, gown_ref, gabove_ref, gsibling_ref, gcross_ref)):

        def merge(i, carry, k=k, target=target):
            at = pl.multiple_of(i * 256, 256)
            value = grad_pos_ref[pl.ds(k * hits + at, 256), :] + grad_neg_ref[
                pl.ds(k * hits + at, 256), :
            ]
            if k == 1:
                value = value + grad_anchor_ref[pl.ds(at, 256), :]
            target[pl.ds(at, 256), :] = value.astype(target.dtype)
            return carry

        lax.fori_loop(0, hits // 256, merge, 0)


def node_backward(
    gradient, hidden_ref, before_ref, agg_ref, w_out, gout_ref, gself_ref, gagg_ref, step
):
    upstream = gradient.astype(BF16)
    hidden = hidden_ref[...]
    hidden_grad = dot(upstream, w_out, 1, 1)
    act_grad = jnp.where(hidden.astype(F32) > 0, hidden_grad, 0.0).astype(BF16)

    @pl.when(step == 0)
    def _():
        gout_ref[...] = jnp.zeros(gout_ref.shape, F32)
        gself_ref[...] = jnp.zeros(gself_ref.shape, F32)
        gagg_ref[...] = jnp.zeros(gagg_ref.shape, F32)

    gout_ref[...] += dot(hidden, upstream, 0, 0)
    gself_ref[...] += dot(before_ref[...], act_grad, 0, 0)
    gagg_ref[...] += dot(agg_ref[...], act_grad, 0, 0)
    return act_grad


def spread_group(index_ref, tiles_ref, adj_ref, agg_grad_t, step, group, slots, rows):
    for g in range(group):
        tile = jnp.concatenate([tiles_ref[g, s] for s in range(slots)], axis=1)
        contrib = dot(agg_grad_t[:, g * rows : (g + 1) * rows], tile, 1, 0)
        for s in range(slots):
            at = index_ref[(step * group + g) * slots + s]
            adj_ref[at] = adj_ref[at] + contrib[:, s * rows : (s + 1) * rows]


def clear_blocks(adj_ref):
    def clear(i, carry):
        adj_ref[i] = jnp.zeros(adj_ref.shape[1:], F32)
        return carry

    lax.fori_loop(0, adj_ref.shape[0], clear, 0)


def last_backward(
    group,
    steps,
    index_ref,
    tiles_ref,
    own_ref,
    down_ref,
    up_ref,
    sib_ref,
    hidden_ref,
    before_ref,
    agg_ref,
    w_self_ref,
    w_agg_ref,
    w_out_ref,
    gout_ref,
    gself_ref,
    gagg_ref,
    direct_ref,
    obelow_ref,
    oown_ref,
    oabove_ref,
    osibling_ref,
    ocross_ref,
    adj_ref,
):
    step = pl.program_id(0)
    slots, rows = tiles_ref.shape[1], tiles_ref.shape[2]

    @pl.when(step == 0)
    def _():
        clear_blocks(adj_ref)

    gradient = own_ref[...] + (
        (down_ref[...].astype(F32) + up_ref[...].astype(F32)) + sib_ref[...].astype(F32)
    )
    act_grad = node_backward(
        gradient, hidden_ref, before_ref, agg_ref, w_out_ref[...], gout_ref, gself_ref, gagg_ref, step
    )
    direct_ref[...] = gradient + dot(act_grad, w_self_ref[...], 1, 1)
    agg_grad_t = dot(w_agg_ref[...], act_grad, 1, 1).astype(BF16)
    spread_group(index_ref, tiles_ref, adj_ref, agg_grad_t, step, group, slots, rows)

    @pl.when(step == steps - 1)
    def _():
        blocks = oown_ref.shape[0]
        for k, target in enumerate((obelow_ref, oown_ref, oabove_ref, osibling_ref, ocross_ref)):

            def store(i, carry, k=k, target=target):
                target[i] = adj_ref[k * blocks + i].astype(target.dtype)
                return carry

            lax.fori_loop(0, blocks, store, 0)


def first_backward(
    group,
    steps,
    index_ref,
    tiles_ref,
    direct_ref,
    own_ref,
    down_ref,
    up_ref,
    sib_ref,
    hidden_ref,
    before_ref,
    agg_ref,
    w_self_ref,
    w_agg_ref,
    w_out_ref,
    feats_ref,
    wcat_ref,
    wcat_t_ref,
    gout_ref,
    gself_ref,
    gagg_ref,
    genc_ref,
    adj_ref,
):
    step = pl.program_id(0)
    slots, rows = tiles_ref.shape[1], tiles_ref.shape[2]
    span = group * rows
    total = feats_ref.shape[1]

    @pl.when(step == 0)
    def _():
        clear_blocks(adj_ref)
        genc_ref[...] = jnp.zeros(genc_ref.shape, F32)

    pieces = []
    for g in range(group):
        returned = own_ref[g] + (
            (down_ref[g].astype(F32) + up_ref[g].astype(F32)) + sib_ref[g].astype(F32)
        )
        pieces.append(returned.T)
    gradient = direct_ref[...] + jnp.concatenate(pieces, axis=0)
    act_grad = node_backward(
        gradient, hidden_ref, before_ref, agg_ref, w_out_ref[...], gout_ref, gself_ref, gagg_ref, step
    )
    direct = gradient + dot(act_grad, w_self_ref[...], 1, 1)
    here = feats_ref[:, pl.ds(pl.multiple_of(total // 5 + step * span, span), span)]
    squashed = jnp.tanh(dot(here, wcat_ref[...], 0, 0))
    genc_ref[...] += dot(here, (direct * (1.0 - squashed * squashed)).astype(BF16), 1, 0)
    agg_grad_t = dot(w_agg_ref[...], act_grad, 1, 1).astype(BF16)
    spread_group(index_ref, tiles_ref, adj_ref, agg_grad_t, step, group, slots, rows)

    @pl.when(step == steps - 1)
    def _():
        per = 4

        def encode(i, carry):
            at = pl.multiple_of(i * (per * rows), per * rows)
            feats = feats_ref[:, pl.ds(at, per * rows)]
            squashed_t = jnp.tanh(dot(wcat_t_ref[...], feats, 1, 0))
            grad_t = jnp.concatenate([adj_ref[i * per + u] for u in range(per)], axis=1)
            grad_t = (grad_t * (1.0 - squashed_t * squashed_t)).astype(BF16)
            return carry + dot(feats, grad_t, 1, 1)

        genc_ref[...] += lax.fori_loop(
            0, total // (per * rows), encode, jnp.zeros(genc_ref.shape, F32)
        )


def body(
    hit_feats,
    layer_ids,
    edge_tiles,
    src_blocks,
    live_slots,
    anchor_hits,
    positive_hits,
    negative_hits,
    w_enc,
    layer_table,
    w_self,
    w_agg,
    w_out,
):
    blocks, slots, rows, _ = edge_tiles.shape
    width = w_enc.shape[1]
    features = hit_feats.shape[0]
    kinds = layer_table.shape[0]
    hits = blocks * rows
    layer_total = w_self.shape[0]
    triplets = anchor_hits.shape[0]
    group = 4
    steps = blocks // group
    span = group * rows
    is_even = lax.rem(lax.axis_index("phi"), 2) == 0

    def place(part):
        odd = jnp.where(is_even, 4, 3)
        near = jnp.where(is_even, 3, 4)
        return jnp.where(
            part == 0,
            0,
            jnp.where(part == 2, 1, jnp.where(part == 4, 2, jnp.where(part == 1, odd, near))),
        )

    live = jnp.arange(slots, dtype=jnp.int32)[None, :] < live_slots[:, None]
    index = jnp.where(
        live, place(src_blocks // blocks) * blocks + src_blocks % blocks, 5 * blocks
    ).reshape(blocks * slots)
    positive = place(positive_hits // hits) * hits + positive_hits % hits
    negative = place(negative_hits // hits) * hits + negative_hits % hits

    pad = -(features + 1) % 16
    packed = jnp.concatenate(
        [hit_feats, layer_ids.astype(BF16)[None, :], jnp.zeros((pad, hits), BF16)], axis=0
    )
    packed = jnp.concatenate(
        [
            permute_far(packed, 2),
            packed,
            permute_far(packed, -2),
            permute_sibling(packed),
            permute_cross(packed),
        ],
        axis=1,
    )
    feature_pad = -features % 16
    onehot = (
        jnp.arange(kinds, dtype=jnp.int32)[:, None].astype(BF16) == packed[features][None, :]
    ).astype(BF16)
    feats = jnp.concatenate(
        [packed[:features], jnp.zeros((feature_pad, 5 * hits), BF16), onehot], axis=0
    )
    wcat = jnp.concatenate([w_enc, jnp.zeros((feature_pad, width), BF16), layer_table], axis=0)
    depth = wcat.shape[0]

    tile_spec = pl.BlockSpec((group, slots, rows, rows), lambda i, *_: (i, 0, 0, 0))
    row_spec = pl.BlockSpec((span, width), lambda i, *_: (i, 0))
    block_spec = pl.BlockSpec((group, width, rows), lambda i, *_: (i, 0, 0))
    weight_spec = full((width, width))
    any_spec = pl.BlockSpec(memory_space=pl.ANY)
    row_shape = jax.ShapeDtypeStruct((hits, width), BF16)
    weight_shape = jax.ShapeDtypeStruct((width, width), F32)

    before0, agg0, hidden0, latents = pl.pallas_call(
        functools.partial(first_forward, group),
        grid_spec=pltpu.PrefetchScalarGridSpec(
            num_scalar_prefetch=1,
            grid=(steps,),
            in_specs=[tile_spec, full((depth, 5 * hits)), full((depth, width))] + [weight_spec] * 3,
            out_specs=[row_spec] * 4,
            scratch_shapes=[pltpu.VMEM((5 * hits + rows, width), BF16)],
        ),
        out_shape=[row_shape] * 4,
        compiler_params=params(),
        name="first_forward",
    )(index, edge_tiles, feats, wcat, w_self[0], w_agg[0], w_out[0])
    stored = [(before0, agg0, hidden0)]
    for layer in range(1, layer_total):
        pieces = window_pieces(latents, is_even)
        aggregated, hidden, updated = pl.pallas_call(
            functools.partial(later_forward, group),
            grid_spec=pltpu.PrefetchScalarGridSpec(
                num_scalar_prefetch=1,
                grid=(steps,),
                in_specs=[tile_spec] + [any_spec] * 5 + [weight_spec] * 3,
                out_specs=[row_spec] * 3,
                scratch_shapes=[
                    pltpu.VMEM((5 * hits + rows, width), BF16),
                    pltpu.SemaphoreType.DMA((5,)),
                ],
            ),
            out_shape=[row_shape] * 3,
            compiler_params=params(),
            name="later_forward",
        )(index, edge_tiles, *pieces, w_self[layer], w_agg[layer], w_out[layer])
        stored.append((latents, aggregated, hidden))
        latents = updated

    pieces = window_pieces(latents, is_even)
    wide_shape = jax.ShapeDtypeStruct((hits, width), F32)
    whole = full((hits, width))
    loss_part, gbelow, gown, gabove, gsibling, gcross = pl.pallas_call(
        functools.partial(contrast_kernel, 1.0 / math.sqrt(width)),
        grid_spec=pltpu.PrefetchScalarGridSpec(
            num_scalar_prefetch=3,
            grid=(1,),
            in_specs=[pl.BlockSpec((hits, width), lambda *_: (0, 0), pipeline_mode=pl.Buffered(1))] * 5,
            out_specs=[full((8, width))]
            + [pl.BlockSpec((hits, width), lambda *_: (0, 0), pipeline_mode=pl.Buffered(1))] * 5,
            scratch_shapes=[pltpu.VMEM((5 * hits, width), F32)] * 3
            + [pltpu.VMEM((hits, width), F32)]
            + [pltpu.VMEM((triplets, width), F32)] * 3,
        ),
        out_shape=[jax.ShapeDtypeStruct((8, width), F32)]
        + [wide_shape] * 3
        + [row_shape] * 2,
        compiler_params=params(),
        name="contrast",
    )(anchor_hits, positive, negative, *pieces)
    down, up, sib = return_pieces(gbelow, gabove, gsibling, gcross, is_even)

    t_shape = jax.ShapeDtypeStruct((blocks, width, rows), F32)
    t_half = jax.ShapeDtypeStruct((blocks, width, rows), BF16)
    t_full = pl.BlockSpec(
        (blocks, width, rows), lambda *_: (0, 0, 0), pipeline_mode=pl.Buffered(1)
    )
    adj_shape = pltpu.VMEM((5 * blocks + 1, width, rows), F32)
    own = gown
    before, aggregated, hidden = stored[1]
    gout1, gself1, gagg1, direct, obelow, own, oabove, osibling, ocross = pl.pallas_call(
        functools.partial(last_backward, group, steps),
        grid_spec=pltpu.PrefetchScalarGridSpec(
            num_scalar_prefetch=1,
            grid=(steps,),
            in_specs=[tile_spec] + [row_spec] * 7 + [weight_spec] * 3,
            out_specs=[weight_spec] * 3 + [row_spec] + [t_full] * 5,
            scratch_shapes=[adj_shape],
        ),
        out_shape=[weight_shape] * 3 + [wide_shape] + [t_shape] * 3 + [t_half] * 2,
        compiler_params=params(),
        name="last_backward",
    )(
        index, edge_tiles, own, down, up, sib, hidden, before, aggregated,
        w_self[1], w_agg[1], w_out[1],
    )
    early = lax.psum(jnp.concatenate([gout1, gself1, gagg1, loss_part], axis=0), "phi")
    down, up, sib = return_pieces(obelow, oabove, osibling, ocross, is_even)
    before, aggregated, hidden = stored[0]
    gout0, gself0, gagg0, genc = pl.pallas_call(
        functools.partial(first_backward, group, steps),
        grid_spec=pltpu.PrefetchScalarGridSpec(
            num_scalar_prefetch=1,
            grid=(steps,),
            in_specs=[tile_spec, row_spec]
            + [block_spec] * 4
            + [row_spec] * 3
            + [weight_spec] * 3
            + [full((depth, 5 * hits)), full((depth, width)), full((width, depth))],
            out_specs=[weight_spec] * 3 + [full((depth, width))],
            scratch_shapes=[adj_shape],
        ),
        out_shape=[weight_shape] * 3 + [jax.ShapeDtypeStruct((depth, width), F32)],
        compiler_params=params(),
        name="first_backward",
    )(
        index, edge_tiles, direct, own, down, up, sib, hidden, before, aggregated,
        w_self[0], w_agg[0], w_out[0], feats, wcat, wcat.T,
    )
    late = lax.psum(jnp.concatenate([gout0, gself0, gagg0, genc], axis=0), "phi")

    triplet_total = triplets * lax.axis_size("phi")
    loss = (early[3 * width, 0] / triplet_total).reshape(1)
    base = 3 * width
    grad_enc = late[base : base + features]
    grad_table = late[base + depth - kinds : base + depth]

    def pair(k):
        return jnp.stack([late[k * width : (k + 1) * width], early[k * width : (k + 1) * width]])

    return (loss, grad_enc, grad_table, pair(1), pair(2), pair(0))


def solution(mesh):
    both = ("event", "phi")
    in_specs = (
        P(None, both),
        P(both),
        P(both, None, None, None),
        P(both, None),
        P(both),
        P(both),
        P(both),
        P(both),
        P(),
        P(),
        P(),
        P(),
        P(),
    )
    out_specs = (
        P("event"),
        P("event", None),
        P("event", None),
        P("event", None, None),
        P("event", None, None),
        P("event", None, None),
    )
    return jax.shard_map(body, mesh=mesh, in_specs=in_specs, out_specs=out_specs, check_vma=False)
```

time: 827 us -> 448 us (0.54)
  other arithmetic: 169 us -> 18.5 us
  local copies, waits for them, and re-layouts: 125 us -> 14.4 us
  Pallas kernels: 0 us -> 97.5 us
  waiting for transfers between devices: 355 us -> 271 us
  blocking collectives: 57.7 us -> 0 us
  matrix products: 51.6 us -> 0 us
  starting transfers between devices: 43 us -> 28.5 us
    ppermute x24 -> x20, waiting for transfers between devices: 355 us -> 182 us  [the longest x10 172 us: permute_far(): lax.ppermute(value, 'phi', [(s, (s + steps) % count) for s in range(count)])]
    scatter-add x5 -> x0, other arithmetic: 144 us -> none  [the longest x2 105 us: block_transpose(): jax.ops.segment_sum(contrib.reshape(block_count * slot_count, block_rows,...]
    pallas_call x0 -> x5, Pallas kernels: none -> 97.5 us  [the longest x1 27.8 us: body(): pl.pallas_call(functools.partial(first_backward, group, steps), grid_spec...]
    psum x1, waiting for transfers between devices: 0.02 us -> 89.2 us  [body(): lax.psum(jnp.concatenate([gout1, gself1, gagg1, loss_part], axis=0), 'phi')]
    psum x1 -> x0, blocking collectives: 57.7 us -> none  [body(): lax.psum((grad_enc, grad_table, jnp.stack(self_grads), jnp.stack(agg_grad...]
    dot_general x26 -> x0, matrix products: 51.6 us -> none  [the longest x2 18.9 us: block_transpose(): jnp.einsum('bsij,biw->bsjw', edge_tiles, agg_grad, preferred_element_type...]
    gather x5 -> x0, local copies, waits for them, and re-layouts: 40.5 us -> none  [the longest x2 22.3 us: block_product(): blocks[src_blocks]]
    reshape x2 -> x1, local copies, waits for them, and re-layouts: 34.9 us -> 0.63 us  [body(): index = jnp.where(live, place(src_blocks // blocks) * blocks + src_blocks...]
  transfers between devices with their start and end apart: 25 -> 21, of which waited for: 12 -> 13; matrix products, arithmetic and copies ran while one was open for 4% -> 4% of each run, Pallas kernels for 0% -> 0%
where the time goes in v1:
time: 448 us; the launch traced here: 446 us
  waiting for transfers between devices  271 us (60%)
  Pallas kernels  97.5 us (22%)
  starting transfers between devices  28.5 us (6%)
  other arithmetic  18.5 us (4%)
  between operations  16.1 us (4%)
  local copies, waits for them, and re-layouts  14.4 us (3%)
    ppermute x10, waiting for transfers between devices, permute_far(): lax.ppermute(value, 'phi', [(s, (s + steps) % count) for s in range(count)])  172 us
    psum x1, waiting for transfers between devices, body(): lax.psum(jnp.concatenate([gout1, gself1, gagg1, loss_part], axis=0), 'phi')  89.2 us
    pallas_call x1, Pallas kernels, body(): pl.pallas_call(functools.partial(first_backward, group, steps), grid_spec...  27.8 us
    ppermute x10, starting transfers between devices, permute_far(): lax.ppermute(value, 'phi', [(s, (s + steps) % count) for s in range(count)])  25.1 us
    pallas_call x1, Pallas kernels, body(): pl.pallas_call(functools.partial(first_forward, group), grid_spec=pltpu.P...  20 us
    pallas_call x1, Pallas kernels, body(): pl.pallas_call(functools.partial(contrast_kernel, 1.0 / math.sqrt(width))...  18.9 us
    pallas_call x1, Pallas kernels, body(): pl.pallas_call(functools.partial(last_backward, group, steps), grid_spec=...  17.6 us
    pallas_call x1, Pallas kernels, body(): pl.pallas_call(functools.partial(later_forward, group), grid_spec=pltpu.P...  13.2 us
  transfers between devices with their start and end apart: 21, of which 13 were waited for; matrix products, arithmetic and copies ran while one was open for 4% of the time, Pallas kernels for 0%

profile of v1, /device:TPU:0, one launch (start us, length us, event | category | flops | bytes accessed | tf_op | source)
XLA Modules:
  0.0 445.9 jit_solution(9507730535868041276)
XLA Ops:
  7.2 0.7 convert_element_type.32
  8.0 0.1 pad.25.clone
  8.0 1.0 maximum_maximum_fusion
  9.0 3.0 collective-permute-start
  12.1 3.1 collective-permute-start.1
  15.2 2.1 collective-permute-start.3
  17.3 0.1 pad.18.clone
  17.3 1.4 slice_bitcast_fusion.8
  18.8 1.5 slice_bitcast_fusion.6
  20.2 1.4 pad_maximum_fusion.6.wcat_ref
  21.6 0.7 fusion.9
  22.3 0.1 copy.28
  22.4 0.6 reshape.27.index_ref
  23.0 1.0 constant_dynamic-update-slice_fusion.3
  24.1 0.3 slice_reduce_fusion
  24.4 0.2 compare_convert_fusion
  24.6 1.3 pad_maximum_fusion.feats_ref
  25.9 20.0 %first_forward.1 = (bf16[4096,128]{1,0:T(8,128)(2,1)}, bf16[4096,128]{1,0:T(8,128)(2,1)}, bf16[4096,128]{1,0:T(8,128)(2,1)}, bf16[4096,128]{1,0:T(8,128)(2,1)}) custom-call(s32[256]{0:T(256)} %reshape.27.index_ref, bf16[32,8,128,128]{3,2,1,0:T(8,128)(2,1)} %tiles_ref.7, bf16[32,20480]{1,0:T(8,128)(2,1)} %pad_maximum_fusion.feats_ref, ...), custom_call_target="tpu_custom_call" | custom-call | tf_op jit(solution)/shard_map/first_forward/pallas_call | solution.py:518
  46.0 4.7 %collective-permute-start.5 = (bf16[4096,128]{1,0:T(8,128)(2,1)}, bf16[4096,128]{1,0:T(8,128)(2,1)S(1)}, u32[]{:S(2)}, u32[]{:S(2)}) collective-permute-start(bf16[4096,128]{1,0:T(8,128)(2,1)} %get-tuple-element.32.own_ref.before_ref), channel_id=1, source_target_pairs={{0,14},{1,15},{2,0},{3,1},{4,2},{5,3},{6,4},{7,5},{8,6},{9,7},{10,... | collective-permute-start | bytes 3145736 | tf_op jit(solution)/shard_map/ppermute | solution.py:35
  50.7 40.0 %collective-permute-done.4.below_ref = bf16[4096,128]{1,0:T(8,128)(2,1)S(1)} collective-permute-done((bf16[4096,128]{1,0:T(8,128)(2,1)}, bf16[4096,128]{1,0:T(8,128)(2,1)S(1)}, u32[]{:S(2)}, u32[]{:S(2)}) %collective-permute-start.4) | collective-permute-done | bytes 1048608 | tf_op jit(solution)/shard_map/ppermute | solution.py:35
  90.7 2.1 collective-permute-done.5.above_ref
  92.8 0.1 broadcast_select_fusion.1
  92.9 0.1 collective-permute-start.7
  93.0 2.6 collective-permute-done.7.cross_ref
  95.7 1.0 copy-done.13
  96.7 13.2 %later_forward.1 = (bf16[4096,128]{1,0:T(8,128)(2,1)}, bf16[4096,128]{1,0:T(8,128)(2,1)}, bf16[4096,128]{1,0:T(8,128)(2,1)}) custom-call(s32[256]{0:T(256)} %reshape.27.index_ref, bf16[32,8,128,128]{3,2,1,0:T(8,128)(2,1)} %tiles_ref.7, bf16[4096,128]{1,0:T(8,128)(2,1)} %copy-done.2, bf16[4096,128]{1,0:T(8,128)(2,1)} %get-tuple-element.32.own_ref.before_ref, ...), custom_call_target="tpu_custom_call" | custom-call | tf_op jit(solution)/shard_map/later_forward/pallas_call | solution.py:534
  109.9 0.3 collective-permute-start.8
  110.2 4.5 collective-permute-start.9
  114.7 41.1 %collective-permute-done.8.below_ref = bf16[4096,128]{1,0:T(8,128)(2,1)S(1)} collective-permute-done((bf16[4096,128]{1,0:T(8,128)(2,1)}, bf16[4096,128]{1,0:T(8,128)(2,1)S(1)}, u32[]{:S(2)}, u32[]{:S(2)}) %collective-permute-start.8) | collective-permute-done | bytes 1048608 | tf_op jit(solution)/shard_map/ppermute | solution.py:35
  155.7 2.9 collective-permute-done.9.above_ref
  158.7 0.1 broadcast_select_fusion
  158.9 0.7 fusion.10
  159.6 1.9 collective-permute-done.11.cross_ref
  161.5 1.0 copy-done.11
  162.5 18.9 %contrast.1 = (f32[8,128]{1,0:T(8,128)}, f32[4096,128]{1,0:T(8,128)}, f32[4096,128]{1,0:T(8,128)}, f32[4096,128]{1,0:T(8,128)}, bf16[4096,128]{1,0:T(8,128)(2,1)}, /*index=5*/bf16[4096,128]{1,0:T(8,128)(2,1)}) custom-call(s32[1024]{0:T(1024)} %anchor_ref.1, s32[1024]{0:T(1024)} %get-tuple-element.76.positive_ref, s32[1024]{0:T(1024)} %get-tuple-element.77.negative_ref, ...), custom_call_target="tpu_custom_call" | custom-call | tf_op jit(solution)/shard_map/contrast/pallas_call | solution.py:556
  181.4 0.1 collective-permute-start.12
  181.5 0.4 collective-permute-start.15
  181.9 2.4 collective-permute-done.12
  184.2 2.7 fusion.3
  187.0 4.7 %collective-permute-start.14 = (bf16[4096,128]{1,0:T(8,128)(2,1)S(1)}, bf16[4096,128]{1,0:T(8,128)(2,1)S(1)}, u32[]{:S(2)}, u32[]{:S(2)}) collective-permute-start(bf16[4096,128]{1,0:T(8,128)(2,1)S(1)} %get-tuple-element.62), channel_id=1, source_target_pairs={{0,14},{1,15},{2,0},{3,1},{4,2},{5,3},{6,4},{7,5},{8,6},{9,7},{10,... | collective-permute-start | bytes 3145736 | tf_op jit(solution)/shard_map/ppermute | solution.py:35
  191.7 40.7 %collective-permute-done.13.down_ref = bf16[4096,128]{1,0:T(8,128)(2,1)S(1)} collective-permute-done((bf16[4096,128]{1,0:T(8,128)(2,1)S(1)}, bf16[4096,128]{1,0:T(8,128)(2,1)S(1)}, u32[]{:S(2)}, u32[]{:S(2)}) %collective-permute-start.13) | collective-permute-done | bytes 1048608 | tf_op jit(solution)/shard_map/ppermute | solution.py:35
  232.5 3.0 collective-permute-done.14.up_ref
  235.5 1.0 copy-done.9
  236.5 17.6 %last_backward.1 = (f32[128,128]{1,0:T(8,128)}, f32[128,128]{1,0:T(8,128)}, f32[128,128]{1,0:T(8,128)}, f32[4096,128]{1,0:T(8,128)}, f32[32,128,128]{2,1,0:T(8,1...) custom-call(s32[256]{0:T(256)} %reshape.27.index_ref, ...), custom_call_target="tpu_custom_call" | custom-call | tf_op jit(solution)/shard_map/last_backward/pallas_call | solution.py:584
  254.2 0.5 collective-permute-start.19
  254.7 2.4 collective-permute-done.16
  257.1 4.2 fusion.7
  261.3 4.7 %collective-permute-start.18 = (bf16[32,128,128]{2,1,0:T(8,128)(2,1)}, bf16[32,128,128]{2,1,0:T(8,128)(2,1)S(1)}, u32[]{:S(2)}, u32[]{:S(2)}) collective-permute-start(bf16[32,128,128]{2,1,0:T(8,128)(2,1)} %get-tuple-element.60), channel_id=1, source_target_pairs={{0,14},{1,15},{2,0},{3,1},{4,2},{5,3},{6,4},{7,5},{8,6},{9,7},{10,... | collective-permute-start | bytes 3145736 | tf_op jit(solution)/shard_map/ppermute | solution.py:35
  266.0 0.7 copy.29
  266.8 0.7 pad_maximum_fusion.2
  267.5 39.6 %collective-permute-done.17.down_ref = bf16[32,128,128]{2,1,0:T(8,128)(2,1)S(1)} collective-permute-done((bf16[32,128,128]{2,1,0:T(8,128)(2,1)}, bf16[32,128,128]{2,1,0:T(8,128)(2,1)S(1)}, u32[]{:S(2)}, u32[]{:S(2)}) %collective-permute-start.17) | collective-permute-done | bytes 1048608 | tf_op jit(solution)/shard_map/ppermute | solution.py:35
  307.1 2.9 collective-permute-done.18.up_ref
  310.0 1.0 copy-done.7
  311.0 27.8 %first_backward.1 = (f32[128,128]{1,0:T(8,128)}, f32[128,128]{1,0:T(8,128)}, f32[128,128]{1,0:T(8,128)}, f32[32,128]{1,0:T(8,128)}) custom-call(s32[256]{0:T(256)} %reshape.27.index_ref, bf16[32,8,128,128]{3,2,1,0:T(8,128)(2,1)} %tiles_ref.7, f32[4096,128]{1,0:T(8,128)} %get-tuple-element.45.direct_ref, f32[32,128,128]{2,1,0:T(8,128)} %get-tuple-element.46.own_ref, ...), custom_call_target="tpu_custom_call" | custom-call | tf_op jit(solution)/shard_map/first_backward/pallas_call | solution.py:603
  338.8 1.6 pad_maximum_fusion.1
  340.5 89.2 %all-reduce.3.cloned.1.call-done = (f32[392,128]{1,0:T(8,128)}, f32[416,128]{1,0:T(8,128)}) async-done(((f32[392,128]{1,0:T(8,128)}, f32[416,128]{1,0:T(8,128)}), (f32[392,128]{1,0:T(8,128)}, f32[416,128]{1,0:T(8,128)})) %all-reduce.3.cloned.1.call-update) | async-done | bytes 413712 | tf_op jit(solution)/shard_map/psum | solution.py:600
  429.6 1.3 slice.77
  430.9 1.3 slice.78
  432.2 1.2 slice.76
  433.4 0.9 slice_bitcast_fusion
  434.3 0.9 slice_bitcast_fusion.1
  435.9 0.7 pad_maximum_fusion.3
  436.6 0.7 pad_maximum_fusion.4
  437.2 0.7 pad_maximum_fusion.5
  (64 shorter events, 0.5 us)
Async XLA Ops:
  7.2 422.5 %all-reduce.3.cloned.1.call-start = ((), (), s32[]{:S(2)}) async-start(), calls=%async_computation | async-start | bytes 827392 | tf_op jit(solution)/shard_map/psum | solution.py:600
  9.0 14.0 %collective-permute-start = (bf16[16,4096]{1,0:T(8,128)(2,1)S(1)}, bf16[16,4096]{1,0:T(8,128)(2,1)S(1)}, u32[]{:S(2)}, u32[]{:S(2)}) collective-permute-start(bf16[16,4096]{1,0:T(8,128)(2,1)S(1)} %maximum_maximum_fusion), channel_id=1, source_target_pairs={{0,2},{1,3},{2,4},{3,5},{4,6},{5,7},{6,8},{7,9},{8,10},{9,11},{10,... | collective-permute-start | bytes 393224 | tf_op jit(solution)/shard_map/ppermute | solution.py:35
  12.1 12.0 %collective-permute-start.1 = (bf16[16,4096]{1,0:T(8,128)(2,1)S(1)}, bf16[16,4096]{1,0:T(8,128)(2,1)S(1)}, u32[]{:S(2)}, u32[]{:S(2)}) collective-permute-start(bf16[16,4096]{1,0:T(8,128)(2,1)S(1)} %maximum_maximum_fusion), channel_id=1, source_target_pairs={{0,14},{1,15},{2,0},{3,1},{4,2},{5,3},{6,4},{7,5},{8,6},{9,7},{10,... | collective-permute-start | bytes 393224 | tf_op jit(solution)/shard_map/ppermute | solution.py:35
  15.2 8.9 %collective-permute-start.2 = (bf16[16,4096]{1,0:T(8,128)(2,1)S(1)}, bf16[16,4096]{1,0:T(8,128)(2,1)S(1)}, u32[]{:S(2)}, u32[]{:S(2)}) collective-permute-start(bf16[16,4096]{1,0:T(8,128)(2,1)S(1)} %maximum_maximum_fusion), channel_id=1, source_target_pairs={{0,1},{1,0},{2,3},{3,2},{4,5},{5,4},{6,7},{7,6},{8,9},{9,8},{10,11... | collective-permute-start | bytes 393224 | tf_op jit(solution)/shard_map/ppermute | solution.py:40
  15.2 8.9 %collective-permute-start.3 = (bf16[16,4096]{1,0:T(8,128)(2,1)S(1)}, bf16[16,4096]{1,0:T(8,128)(2,1)S(1)}, u32[]{:S(2)}, u32[]{:S(2)}) collective-permute-start(bf16[16,4096]{1,0:T(8,128)(2,1)S(1)} %maximum_maximum_fusion), channel_id=1, source_target_pairs={{0,15},{1,2},{2,1},{3,4},{4,3},{5,6},{6,5},{7,8},{8,7},{9,10},{10,... | collective-permute-start | bytes 393224 | tf_op jit(solution)/shard_map/ppermute | solution.py:45
  46.0 44.8 %collective-permute-start.4 = (bf16[4096,128]{1,0:T(8,128)(2,1)}, bf16[4096,128]{1,0:T(8,128)(2,1)S(1)}, u32[]{:S(2)}, u32[]{:S(2)}) collective-permute-start(bf16[4096,128]{1,0:T(8,128)(2,1)} %get-tuple-element.32.own_ref.before_ref), channel_id=1, source_target_pairs={{0,2},{1,3},{2,4},{3,5},{4,6},{5,7},{6,8},{7,9},{8,10},{9,11},{10,... | collective-permute-start | bytes 3145736 | tf_op jit(solution)/shard_map/ppermute | solution.py:35
  46.0 46.8 %collective-permute-start.5 = (bf16[4096,128]{1,0:T(8,128)(2,1)}, bf16[4096,128]{1,0:T(8,128)(2,1)S(1)}, u32[]{:S(2)}, u32[]{:S(2)}) collective-permute-start(bf16[4096,128]{1,0:T(8,128)(2,1)} %get-tuple-element.32.own_ref.before_ref), channel_id=1, source_target_pairs={{0,14},{1,15},{2,0},{3,1},{4,2},{5,3},{6,4},{7,5},{8,6},{9,7},{10,... | collective-permute-start | bytes 3145736 | tf_op jit(solution)/shard_map/ppermute | solution.py:35
  50.7 42.3 %collective-permute-start.6 = (bf16[4096,128]{1,0:T(8,128)(2,1)}, bf16[4096,128]{1,0:T(8,128)(2,1)S(1)}, u32[]{:S(2)}, u32[]{:S(2)}) collective-permute-start(bf16[4096,128]{1,0:T(8,128)(2,1)} %get-tuple-element.32.own_ref.before_ref), channel_id=1, source_target_pairs={{0,1},{1,0},{2,3},{3,2},{4,5},{5,4},{6,7},{7,6},{8,9},{9,8},{10,11... | collective-permute-start | bytes 3145736 | tf_op jit(solution)/shard_map/ppermute | solution.py:40
  90.7 6.0 %copy-start.2 = (bf16[4096,128]{1,0:T(8,128)(2,1)}, bf16[4096,128]{1,0:T(8,128)(2,1)S(1)}, u32[]{:S(2)}) copy-start(bf16[4096,128]{1,0:T(8,128)(2,1)S(1)} %collective-permute-done.4.below_ref) | copy-start | bytes 3145732
  92.8 3.8 copy-start.3
  92.9 2.7 collective-permute-start.7
  93.0 3.6 copy-start.12
  95.7 1.0 copy-start.13
  109.9 49.0 %copy-start.19 = (s32[1024]{0:T(1024)S(1)}, s32[1024]{0:T(1024)}, u32[]{:S(2)}) copy-start(s32[1024]{0:T(1024)} %param.19) | copy-start | bytes 12292
  109.9 49.0 %copy-start.20 = (s32[1024]{0:T(1024)S(1)}, s32[1024]{0:T(1024)}, u32[]{:S(2)}) copy-start(s32[1024]{0:T(1024)} %param.20) | copy-start | bytes 12292
  109.9 45.8 %collective-permute-start.8 = (bf16[4096,128]{1,0:T(8,128)(2,1)}, bf16[4096,128]{1,0:T(8,128)(2,1)S(1)}, u32[]{:S(2)}, u32[]{:S(2)}) collective-permute-start(bf16[4096,128]{1,0:T(8,128)(2,1)} %get-tuple-element.33.own_ref), channel_id=1, source_target_pairs={{0,2},{1,3},{2,4},{3,5},{4,6},{5,7},{6,8},{7,9},{8,10},{9,11},{10,... | collective-permute-start | bytes 3145736 | tf_op jit(solution)/shard_map/ppermute | solution.py:35
  110.2 48.4 %collective-permute-start.9 = (bf16[4096,128]{1,0:T(8,128)(2,1)}, bf16[4096,128]{1,0:T(8,128)(2,1)S(1)}, u32[]{:S(2)}, u32[]{:S(2)}) collective-permute-start(bf16[4096,128]{1,0:T(8,128)(2,1)} %get-tuple-element.33.own_ref), channel_id=1, source_target_pairs={{0,14},{1,15},{2,0},{3,1},{4,2},{5,3},{6,4},{7,5},{8,6},{9,7},{10,... | collective-permute-start | bytes 3145736 | tf_op jit(solution)/shard_map/ppermute | solution.py:35
  114.7 44.9 %collective-permute-start.10 = (bf16[4096,128]{1,0:T(8,128)(2,1)}, bf16[4096,128]{1,0:T(8,128)(2,1)S(1)}, u32[]{:S(2)}, u32[]{:S(2)}) collective-permute-start(bf16[4096,128]{1,0:T(8,128)(2,1)} %get-tuple-element.33.own_ref), channel_id=1, source_target_pairs={{0,1},{1,0},{2,3},{3,2},{4,5},{5,4},{6,7},{7,6},{8,9},{9,8},{10,11... | collective-permute-start | bytes 3145736 | tf_op jit(solution)/shard_map/ppermute | solution.py:40
  155.7 6.8 %copy-start = (bf16[4096,128]{1,0:T(8,128)(2,1)}, bf16[4096,128]{1,0:T(8,128)(2,1)S(1)}, u32[]{:S(2)}) copy-start(bf16[4096,128]{1,0:T(8,128)(2,1)S(1)} %collective-permute-done.8.below_ref) | copy-start | bytes 3145732
  158.7 3.8 copy-start.1
  158.8 2.7 collective-permute-start.11
  159.6 2.9 copy-start.10
  161.5 1.0 copy-start.11
  181.4 2.9 collective-permute-start.12
  181.5 10.2 %collective-permute-start.15 = (bf16[4096,128]{1,0:T(8,128)(2,1)}, bf16[4096,128]{1,0:T(8,128)(2,1)S(1)}, u32[]{:S(2)}, u32[]{:S(2)}) collective-permute-start(bf16[4096,128]{1,0:T(8,128)(2,1)} %get-tuple-element.38), channel_id=1, source_target_pairs={{0,1},{1,0},{2,3},{3,2},{4,5},{5,4},{6,7},{7,6},{8,9},{9,8},{10,11... | collective-permute-start | bytes 3145736 | tf_op jit(solution)/shard_map/ppermute | solution.py:40
  186.9 45.5 %collective-permute-start.13 = (bf16[4096,128]{1,0:T(8,128)(2,1)S(1)}, bf16[4096,128]{1,0:T(8,128)(2,1)S(1)}, u32[]{:S(2)}, u32[]{:S(2)}) collective-permute-start(bf16[4096,128]{1,0:T(8,128)(2,1)S(1)} %get-tuple-element.63), channel_id=1, source_target_pairs={{0,2},{1,3},{2,4},{3,5},{4,6},{5,7},{6,8},{7,9},{8,10},{9,11},{10,... | collective-permute-start | bytes 3145736 | tf_op jit(solution)/shard_map/ppermute | solution.py:35
  187.0 48.5 %collective-permute-start.14 = (bf16[4096,128]{1,0:T(8,128)(2,1)S(1)}, bf16[4096,128]{1,0:T(8,128)(2,1)S(1)}, u32[]{:S(2)}, u32[]{:S(2)}) collective-permute-start(bf16[4096,128]{1,0:T(8,128)(2,1)S(1)} %get-tuple-element.62), channel_id=1, source_target_pairs={{0,14},{1,15},{2,0},{3,1},{4,2},{5,3},{6,4},{7,5},{8,6},{9,7},{10,... | collective-permute-start | bytes 3145736 | tf_op jit(solution)/shard_map/ppermute | solution.py:35
  191.7 43.8 %copy-start.5 = (bf16[4096,128]{1,0:T(8,128)(2,1)}, bf16[4096,128]{1,0:T(8,128)(2,1)S(1)}, u32[]{:S(2)}) copy-start(bf16[4096,128]{1,0:T(8,128)(2,1)S(1)} %collective-permute-done.15.sib_ref) | copy-start | bytes 3145732
  232.5 3.1 copy-start.8
  235.5 1.0 copy-start.9
  254.1 2.9 collective-permute-start.16
  254.2 13.3 %collective-permute-start.19 = (bf16[32,128,128]{2,1,0:T(8,128)(2,1)}, bf16[32,128,128]{2,1,0:T(8,128)(2,1)S(1)}, u32[]{:S(2)}, u32[]{:S(2)}) collective-permute-start(bf16[32,128,128]{2,1,0:T(8,128)(2,1)} %get-tuple-element.50), channel_id=1, source_target_pairs={{0,1},{1,0},{2,3},{3,2},{4,5},{5,4},{6,7},{7,6},{8,9},{9,8},{10,11... | collective-permute-start | bytes 3145736 | tf_op jit(solution)/shard_map/ppermute | solution.py:40
  257.0 9.0 %copy-start.14 = (bf16[32,128]{1,0:T(8,128)(2,1)S(1)}, bf16[32,128]{1,0:T(8,128)(2,1)}, u32[]{:S(2)}) copy-start(bf16[32,128]{1,0:T(8,128)(2,1)} %pad_maximum_fusion.6.wcat_ref) | copy-start | bytes 24580
  257.0 9.7 %copy-start.15 = (f32[128,128]{1,0:T(8,128)S(1)}, f32[128,128]{1,0:T(8,128)}, u32[]{:S(2)}) copy-start(f32[128,128]{1,0:T(8,128)} %get-tuple-element.41) | copy-start | bytes 196612
  257.0 9.7 %copy-start.16 = (f32[128,128]{1,0:T(8,128)S(1)}, f32[128,128]{1,0:T(8,128)}, u32[]{:S(2)}) copy-start(f32[128,128]{1,0:T(8,128)} %get-tuple-element.42) | copy-start | bytes 196612
  257.0 9.7 %copy-start.17 = (f32[128,128]{1,0:T(8,128)S(1)}, f32[128,128]{1,0:T(8,128)}, u32[]{:S(2)}) copy-start(f32[128,128]{1,0:T(8,128)} %get-tuple-element.43) | copy-start | bytes 196612
  257.1 9.7 %copy-start.18 = (f32[8,128]{1,0:T(8,128)S(1)}, f32[8,128]{1,0:T(8,128)}, u32[]{:S(2)}) copy-start(f32[8,128]{1,0:T(8,128)} %get-tuple-element.44) | copy-start | bytes 12292
  261.3 45.8 %collective-permute-start.17 = (bf16[32,128,128]{2,1,0:T(8,128)(2,1)}, bf16[32,128,128]{2,1,0:T(8,128)(2,1)S(1)}, u32[]{:S(2)}, u32[]{:S(2)}) collective-permute-start(bf16[32,128,128]{2,1,0:T(8,128)(2,1)} %get-tuple-element.61), channel_id=1, source_target_pairs={{0,2},{1,3},{2,4},{3,5},{4,6},{5,7},{6,8},{7,9},{8,10},{9,11},{10,... | collective-permute-start | bytes 3145736 | tf_op jit(solution)/shard_map/ppermute | solution.py:35
  261.3 48.7 %collective-permute-start.18 = (bf16[32,128,128]{2,1,0:T(8,128)(2,1)}, bf16[32,128,128]{2,1,0:T(8,128)(2,1)S(1)}, u32[]{:S(2)}, u32[]{:S(2)}) collective-permute-start(bf16[32,128,128]{2,1,0:T(8,128)(2,1)} %get-tuple-element.60), channel_id=1, source_target_pairs={{0,14},{1,15},{2,0},{3,1},{4,2},{5,3},{6,4},{7,5},{8,6},{9,7},{10,... | collective-permute-start | bytes 3145736 | tf_op jit(solution)/shard_map/ppermute | solution.py:35
  267.5 42.6 %copy-start.4 = (bf16[32,128,128]{2,1,0:T(8,128)(2,1)}, bf16[32,128,128]{2,1,0:T(8,128)(2,1)S(1)}, u32[]{:S(2)}) copy-start(bf16[32,128,128]{2,1,0:T(8,128)(2,1)S(1)} %collective-permute-done.19.sib_ref) | copy-start | bytes 3145732
  307.1 3.0 copy-start.6
  310.0 1.0 copy-start.7
Sparse Core Ops, SparseCore 0:
  340.6 88.9 all-reduce.2

commit v2 on v1

--- a/solution.py
+++ b/solution.py
@@ -30,43 +30,287 @@
     )
 
 
-def permute_far(value, steps):
+CHUNKS = 8
+
+
+def permute(value, target_of):
     count = lax.axis_size("phi")
-    return lax.ppermute(value, "phi", [(s, (s + steps) % count) for s in range(count)])
-
-
-def permute_sibling(value):
+    return lax.ppermute(value, "phi", [(s, target_of(s) % count) for s in range(count)])
+
+
+def direct_target(s):
+    return s ^ 2
+
+
+def relayed_target(s):
+    return s + 2 if (s // 2) % 2 else s - 2
+
+
+def sibling_target(s):
+    return s ^ 1
+
+
+def cross_target(s):
+    return s + 1 if s % 2 else s - 1
+
+
+def peers():
     count = lax.axis_size("phi")
-    return lax.ppermute(value, "phi", [(s, s ^ 1) for s in range(count)])
-
-
-def permute_cross(value):
-    count = lax.axis_size("phi")
-    return lax.ppermute(
-        value, "phi", [(s, (s + (1 if s % 2 else -1)) % count) for s in range(count)]
-    )
-
-
-def window_pieces(latents, is_even):
-    below = permute_far(latents, 2)
-    above = permute_far(latents, -2)
-    sibling = permute_sibling(latents)
-    cross = permute_sibling(jnp.where(is_even, above, below))
-    return below, latents, above, sibling, cross
-
-
-def return_pieces(below, above, sibling, cross, is_even):
-    cross_in = permute_sibling(cross).astype(F32)
-    sibling_in = permute_sibling(sibling)
-    zero = jnp.zeros((), F32)
-    above_out = (above + jnp.where(is_even, cross_in, zero)).astype(BF16)
-    below_out = (below + jnp.where(is_even, zero, cross_in)).astype(BF16)
-    from_below = permute_far(above_out, 2)
-    from_above = permute_far(below_out, -2)
-    return from_below, from_above, sibling_in
-
-
-def aggregate_group(index_ref, tiles_ref, window_ref, step, group, slots, rows, zero_ok=None):
+    me = lax.axis_index("phi")
+    odd_pair = (me // 2) % 2
+    odd_core = me % 2
+    direct = me + 2 - 4 * odd_pair
+    sibling = me + 1 - 2 * odd_core
+    stride = 4 - 8 * odd_pair
+    onward = (me + stride + count) % count
+    source = (me - stride + count) % count
+    return direct, sibling, onward, source, odd_pair == odd_core
+
+
+def remote(src, dst, send, recv, target):
+    return pltpu.make_async_remote_copy(
+        src_ref=src,
+        dst_ref=dst,
+        send_sem=send,
+        recv_sem=recv,
+        device_id={"phi": target},
+        device_id_type=pl.DeviceIdType.MESH,
+    )
+
+
+def greet(targets):
+    barrier = pltpu.get_barrier_semaphore()
+    for target in targets:
+        pl.semaphore_signal(
+            barrier, inc=1, device_id={"phi": target}, device_id_type=pl.DeviceIdType.MESH
+        )
+    pl.semaphore_wait(barrier, len(targets))
+
+
+def exchange_kernel(own, direct_out, relay_out, sib_out, cross_out, *sems):
+    ys, yr, zs, zr, cs, cr, ss, sr = sems
+    direct, sibling, onward, source, direct_crosses = peers()
+    size = own.shape[0] // CHUNKS
+    greet((direct, sibling, source))
+
+    def part(ref, i):
+        return ref.at[pl.ds(i * size, size)]
+
+    first = [
+        remote(part(own, i), part(direct_out, i), ys.at[i], yr.at[i], direct) for i in range(CHUNKS)
+    ]
+    second = [
+        remote(part(direct_out, i), part(relay_out, i), zs.at[i], zr.at[i], onward)
+        for i in range(CHUNKS)
+    ]
+    cross_a = [
+        remote(part(direct_out, i), part(cross_out, i), cs.at[i], cr.at[i], sibling)
+        for i in range(CHUNKS)
+    ]
+    cross_b = [
+        remote(part(relay_out, i), part(cross_out, i), cs.at[i], cr.at[i], sibling)
+        for i in range(CHUNKS)
+    ]
+    near = remote(own, sib_out, ss.at[0], sr.at[0], sibling)
+    for copy in first:
+        copy.start()
+    near.start()
+    for i in range(CHUNKS):
+        first[i].wait_recv()
+        second[i].start()
+
+        @pl.when(direct_crosses)
+        def _():
+            cross_a[i].start()
+
+    for i in range(CHUNKS):
+        second[i].wait_recv()
+
+        @pl.when(jnp.logical_not(direct_crosses))
+        def _():
+            cross_b[i].start()
+
+    near.wait()
+    for i in range(CHUNKS):
+        first[i].wait_send()
+        second[i].wait_send()
+        cross_a[i].wait()
+
+
+def window_pieces(latents):
+    hits, width = latents.shape
+    any_spec = pl.BlockSpec(memory_space=pl.ANY)
+    direct, relayed, sibling, cross = pl.pallas_call(
+        exchange_kernel,
+        in_specs=[any_spec],
+        out_specs=[any_spec] * 4,
+        out_shape=[jax.ShapeDtypeStruct((hits, width), BF16)] * 4,
+        scratch_shapes=[pltpu.SemaphoreType.DMA((CHUNKS,))] * 6 + [pltpu.SemaphoreType.DMA((1,))] * 2,
+        compiler_params=pltpu.CompilerParams(collective_id=1, has_side_effects=True),
+        name="exchange",
+    )(latents)
+    return direct, latents, relayed, sibling, cross
+
+
+def return_kernel(
+    direct_ref,
+    relay_ref,
+    sib_ref,
+    cross_ref,
+    total_out,
+    sib_out,
+    cross_in,
+    relay_send,
+    relay_in,
+    direct_send,
+    *sems,
+):
+    ys, yr, zs, zr, cs, cr, ss, sr = sems
+    direct, sibling, onward, source, to_direct = peers()
+    size = direct_ref.shape[0] // CHUNKS
+    greet((direct, sibling, onward))
+
+    def rows(i):
+        return pl.ds(i * size, size)
+
+    crosses = [
+        remote(cross_ref.at[rows(i)], cross_in.at[rows(i)], cs.at[i], cr.at[i], sibling)
+        for i in range(CHUNKS)
+    ]
+    first = [
+        remote(relay_send.at[rows(i)], relay_in.at[rows(i)], zs.at[i], zr.at[i], source)
+        for i in range(CHUNKS)
+    ]
+    second = [
+        remote(direct_send.at[rows(i)], total_out.at[rows(i)], ys.at[i], yr.at[i], direct)
+        for i in range(CHUNKS)
+    ]
+    near = remote(sib_ref, sib_out, ss.at[0], sr.at[0], sibling)
+    for copy in crosses:
+        copy.start()
+    near.start()
+    for i in range(CHUNKS):
+        crosses[i].wait_recv()
+        extra = jnp.where(to_direct, 0.0, cross_in[rows(i), :].astype(F32))
+        relay_send[rows(i), :] = (relay_ref[rows(i), :] + extra).astype(BF16)
+        first[i].start()
+    for i in range(CHUNKS):
+        first[i].wait_recv()
+        extra = jnp.where(to_direct, cross_in[rows(i), :].astype(F32), 0.0)
+        direct_send[rows(i), :] = (
+            direct_ref[rows(i), :] + extra + relay_in[rows(i), :].astype(F32)
+        ).astype(BF16)
+        second[i].start()
+    near.wait()
+    for i in range(CHUNKS):
+        crosses[i].wait_send()
+        first[i].wait_send()
+        second[i].wait()
+
+
+def return_pieces(direct, relayed, sibling, cross):
+    shape = sibling.shape
+    hits, width = math.prod(shape[:-1]), shape[-1]
+    vmem = pl.BlockSpec(memory_space=pltpu.VMEM)
+    half = jax.ShapeDtypeStruct((hits, width), BF16)
+    total, sib = pl.pallas_call(
+        return_kernel,
+        in_specs=[vmem] * 4,
+        out_specs=[vmem] * 2,
+        out_shape=[half] * 2,
+        scratch_shapes=[pltpu.VMEM((hits, width), BF16)] * 4
+        + [pltpu.SemaphoreType.DMA((CHUNKS,))] * 6
+        + [pltpu.SemaphoreType.DMA((1,))] * 2,
+        compiler_params=pltpu.CompilerParams(
+            collective_id=2, has_side_effects=True, vmem_limit_bytes=VMEM_BYTES
+        ),
+        name="give_back",
+    )(*[piece.reshape(hits, width) for piece in (direct, relayed, sibling, cross)])
+    return total.reshape(shape), sib.reshape(shape)
+
+
+def sum_kernel(
+    pairs, x_ref, out_ref, half_in, acc_ref, slots_in, all_ref, s0, r0, s1, r1, s2, r2, s3, r3
+):
+    me = lax.axis_index("phi")
+    pair, core = me // 2, me % 2
+    sibling = me + 1 - 2 * core
+    half = x_ref.shape[0] // 2
+    chunk = half // pairs
+    others = [((pair + d) % pairs) * 2 + core for d in range(1, pairs)]
+    greet([sibling] + others)
+
+    def span(start, size):
+        return pl.ds(pl.multiple_of(start, 8), size)
+
+    swap = remote(x_ref.at[span((1 - core) * half, half)], half_in, s0.at[0], r0.at[0], sibling)
+    swap.start()
+    swap.wait()
+    acc_ref[...] = x_ref[span(core * half, half), :] + half_in[...]
+    scatter = [
+        remote(
+            acc_ref.at[span(((pair + d) % pairs) * chunk, chunk)],
+            slots_in.at[d - 1],
+            s1.at[d - 1],
+            r1.at[d - 1],
+            others[d - 1],
+        )
+        for d in range(1, pairs)
+    ]
+    for copy in scatter:
+        copy.start()
+    total = acc_ref[span(pair * chunk, chunk), :]
+    for d in range(1, pairs):
+        scatter[d - 1].wait_recv()
+        total = total + slots_in[d - 1]
+    mine = span(core * half + pair * chunk, chunk)
+    all_ref[mine, :] = total
+    gather = [
+        remote(all_ref.at[mine], all_ref.at[mine], s2.at[d - 1], r2.at[d - 1], others[d - 1])
+        for d in range(1, pairs)
+    ]
+    for copy in gather:
+        copy.start()
+    for copy in gather:
+        copy.wait()
+    for copy in scatter:
+        copy.wait_send()
+    whole = span(core * half, half)
+    last = remote(all_ref.at[whole], all_ref.at[whole], s3.at[0], r3.at[0], sibling)
+    last.start()
+    last.wait()
+    out_ref[...] = all_ref[...]
+
+
+def sum_all(value):
+    pairs = lax.axis_size("phi") // 2
+    rows, width = value.shape
+    chunk = -(-rows // (16 * pairs)) * 8
+    total = 2 * pairs * chunk
+    value = jnp.concatenate([value, jnp.zeros((total - rows, width), F32)], axis=0)
+    vmem = pl.BlockSpec(memory_space=pltpu.VMEM)
+    one = pltpu.SemaphoreType.DMA((1,))
+    many = pltpu.SemaphoreType.DMA((pairs - 1,))
+    return pl.pallas_call(
+        functools.partial(sum_kernel, pairs),
+        in_specs=[vmem],
+        out_specs=vmem,
+        out_shape=jax.ShapeDtypeStruct((total, width), F32),
+        scratch_shapes=[
+            pltpu.VMEM((total // 2, width), F32),
+            pltpu.VMEM((total // 2, width), F32),
+            pltpu.VMEM((pairs - 1, chunk, width), F32),
+            pltpu.VMEM((total, width), F32),
+            one, one, many, many, many, many, one, one,
+        ],
+        compiler_params=pltpu.CompilerParams(
+            collective_id=3, has_side_effects=True, vmem_limit_bytes=VMEM_BYTES
+        ),
+        name="sum_all",
+    )(value)
+
+
+def aggregate_group(index_ref, tiles_ref, window_ref, step, group, slots, rows):
     results = []
     for g in range(group):
         tile = jnp.concatenate([tiles_ref[g, s] for s in range(slots)], axis=1)
@@ -322,8 +566,7 @@
     index_ref,
     tiles_ref,
     own_ref,
-    down_ref,
-    up_ref,
+    total_ref,
     sib_ref,
     hidden_ref,
     before_ref,
@@ -350,7 +593,7 @@
         clear_blocks(adj_ref)
 
     gradient = own_ref[...] + (
-        (down_ref[...].astype(F32) + up_ref[...].astype(F32)) + sib_ref[...].astype(F32)
+        total_ref[...].astype(F32) + sib_ref[...].astype(F32)
     )
     act_grad = node_backward(
         gradient, hidden_ref, before_ref, agg_ref, w_out_ref[...], gout_ref, gself_ref, gagg_ref, step
@@ -378,8 +621,7 @@
     tiles_ref,
     direct_ref,
     own_ref,
-    down_ref,
-    up_ref,
+    total_ref,
     sib_ref,
     hidden_ref,
     before_ref,
@@ -409,7 +651,7 @@
     pieces = []
     for g in range(group):
         returned = own_ref[g] + (
-            (down_ref[g].astype(F32) + up_ref[g].astype(F32)) + sib_ref[g].astype(F32)
+            total_ref[g].astype(F32) + sib_ref[g].astype(F32)
         )
         pieces.append(returned.T)
     gradient = direct_ref[...] + jnp.concatenate(pieces, axis=0)
@@ -465,16 +707,19 @@
     group = 4
     steps = blocks // group
     span = group * rows
-    is_even = lax.rem(lax.axis_index("phi"), 2) == 0
+    me = lax.axis_index("phi")
+    is_even = me % 2 == 0
+    even_pair = (me // 2) % 2 == 0
 
     def place(part):
-        odd = jnp.where(is_even, 4, 3)
-        near = jnp.where(is_even, 3, 4)
-        return jnp.where(
-            part == 0,
-            0,
-            jnp.where(part == 2, 1, jnp.where(part == 4, 2, jnp.where(part == 1, odd, near))),
+        spots = (
+            jnp.where(even_pair, 2, 0),
+            jnp.where(is_even, 4, 3),
+            1,
+            jnp.where(is_even, 3, 4),
+            jnp.where(even_pair, 0, 2),
         )
+        return sum(jnp.where(part == k, spot, 0) for k, spot in enumerate(spots))
 
     live = jnp.arange(slots, dtype=jnp.int32)[None, :] < live_slots[:, None]
     index = jnp.where(
@@ -489,11 +734,11 @@
     )
     packed = jnp.concatenate(
         [
-            permute_far(packed, 2),
+            permute(packed, direct_target),
             packed,
-            permute_far(packed, -2),
-            permute_sibling(packed),
-            permute_cross(packed),
+            permute(packed, relayed_target),
+            permute(packed, sibling_target),
+            permute(packed, cross_target),
         ],
         axis=1,
     )
@@ -530,7 +775,7 @@
     )(index, edge_tiles, feats, wcat, w_self[0], w_agg[0], w_out[0])
     stored = [(before0, agg0, hidden0)]
     for layer in range(1, layer_total):
-        pieces = window_pieces(latents, is_even)
+        pieces = window_pieces(latents)
         aggregated, hidden, updated = pl.pallas_call(
             functools.partial(later_forward, group),
             grid_spec=pltpu.PrefetchScalarGridSpec(
@@ -550,7 +795,7 @@
         stored.append((latents, aggregated, hidden))
         latents = updated
 
-    pieces = window_pieces(latents, is_even)
+    pieces = window_pieces(latents)
     wide_shape = jax.ShapeDtypeStruct((hits, width), F32)
     whole = full((hits, width))
     loss_part, gbelow, gown, gabove, gsibling, gcross = pl.pallas_call(
@@ -571,7 +816,7 @@
         compiler_params=params(),
         name="contrast",
     )(anchor_hits, positive, negative, *pieces)
-    down, up, sib = return_pieces(gbelow, gabove, gsibling, gcross, is_even)
+    total, sib = return_pieces(gbelow, gabove, gsibling, gcross)
 
     t_shape = jax.ShapeDtypeStruct((blocks, width, rows), F32)
     t_half = jax.ShapeDtypeStruct((blocks, width, rows), BF16)
@@ -586,7 +831,7 @@
         grid_spec=pltpu.PrefetchScalarGridSpec(
             num_scalar_prefetch=1,
             grid=(steps,),
-            in_specs=[tile_spec] + [row_spec] * 7 + [weight_spec] * 3,
+            in_specs=[tile_spec] + [row_spec] * 6 + [weight_spec] * 3,
             out_specs=[weight_spec] * 3 + [row_spec] + [t_full] * 5,
             scratch_shapes=[adj_shape],
         ),
@@ -594,11 +839,10 @@
         compiler_params=params(),
         name="last_backward",
     )(
-        index, edge_tiles, own, down, up, sib, hidden, before, aggregated,
+        index, edge_tiles, own, total, sib, hidden, before, aggregated,
         w_self[1], w_agg[1], w_out[1],
     )
-    early = lax.psum(jnp.concatenate([gout1, gself1, gagg1, loss_part], axis=0), "phi")
-    down, up, sib = return_pieces(obelow, oabove, osibling, ocross, is_even)
+    total, sib = return_pieces(obelow, oabove, osibling, ocross)
     before, aggregated, hidden = stored[0]
     gout0, gself0, gagg0, genc = pl.pallas_call(
         functools.partial(first_backward, group, steps),
@@ -606,7 +850,7 @@
             num_scalar_prefetch=1,
             grid=(steps,),
             in_specs=[tile_spec, row_spec]
-            + [block_spec] * 4
+            + [block_spec] * 3
             + [row_spec] * 3
             + [weight_spec] * 3
             + [full((depth, 5 * hits)), full((depth, width)), full((width, depth))],
@@ -617,19 +861,21 @@
         compiler_params=params(),
         name="first_backward",
     )(
-        index, edge_tiles, direct, own, down, up, sib, hidden, before, aggregated,
+        index, edge_tiles, direct, own, total, sib, hidden, before, aggregated,
         w_self[0], w_agg[0], w_out[0], feats, wcat, wcat.T,
     )
-    late = lax.psum(jnp.concatenate([gout0, gself0, gagg0, genc], axis=0), "phi")
+    late = sum_all(
+        jnp.concatenate([gout0, gout1, gself0, gself1, gagg0, gagg1, genc, loss_part], axis=0)
+    )
 
     triplet_total = triplets * lax.axis_size("phi")
-    loss = (early[3 * width, 0] / triplet_total).reshape(1)
-    base = 3 * width
+    base = 6 * width
+    loss = (late[base + depth, 0] / triplet_total).reshape(1)
     grad_enc = late[base : base + features]
     grad_table = late[base + depth - kinds : base + depth]
 
     def pair(k):
-        return jnp.stack([late[k * width : (k + 1) * width], early[k * width : (k + 1) * width]])
+        return late[2 * k * width : 2 * (k + 1) * width].reshape(layer_total, width, width)
 
     return (loss, grad_enc, grad_table, pair(1), pair(2), pair(0))
 

time: 448 us -> 289 us (0.65)
  waiting for transfers between devices: 271 us -> 0.01 us
  Pallas kernels: 97.5 us -> 255 us
  starting transfers between devices: 28.5 us -> 7.9 us
  between operations: 16.1 us -> 2.61 us
  other arithmetic: 18.5 us -> 7.09 us
    ppermute x20 -> x4, waiting for transfers between devices: 182 us -> 0.01 us  [permute(): lax.ppermute(value, 'phi', [(s, target_of(s) % count) for s in range(coun...]
    pallas_call x0 -> x5, Pallas kernels: none -> 158 us  [the longest x2 73.2 us: return_pieces(): pl.pallas_call(return_kernel, in_specs=[vmem] * 4, out_specs=[vmem] * 2,...]
    psum x1 -> x0, waiting for transfers between devices: 89.2 us -> none  [body(): lax.psum(jnp.concatenate([gout1, gself1, gagg1, loss_part], axis=0), 'phi')]
    ppermute x20 -> x4, starting transfers between devices: 28.4 us -> 7.9 us  [permute(): lax.ppermute(value, 'phi', [(s, target_of(s) % count) for s in range(coun...]
    convert_element_type x2 -> x0, other arithmetic: 6.93 us -> none  [return_pieces(): below_out = (below + jnp.where(is_even, zero, cross_in)).astype(BF16)]
  transfers between devices with their start and end apart: 21 -> 4, of which waited for: 13 -> 0; matrix products, arithmetic and copies ran while one was open for 4% -> 3% of each run, Pallas kernels for 0% -> 0%
where the time goes in v2:
time: 289 us; the launch traced here: 287 us
  Pallas kernels  255 us (88%)
  local copies, waits for them, and re-layouts  14.4 us (5%)
  starting transfers between devices  7.9 us (3%)
  other arithmetic  7.09 us (2%)
    pallas_call x2, Pallas kernels, return_pieces(): pl.pallas_call(return_kernel, in_specs=[vmem] * 4, out_specs=[vmem] * 2,...  73.2 us
    pallas_call x2, Pallas kernels, window_pieces(): pl.pallas_call(exchange_kernel, in_specs=[any_spec], out_specs=[any_spec]...  65.8 us
    pallas_call x1, Pallas kernels, body(): pl.pallas_call(functools.partial(first_backward, group, steps), grid_spec...  27.8 us
    pallas_call x1, Pallas kernels, body(): pl.pallas_call(functools.partial(first_forward, group), grid_spec=pltpu.P...  20 us
    pallas_call x1, Pallas kernels, sum_all(): pl.pallas_call(functools.partial(sum_kernel, pairs), in_specs=[vmem], out...  18.9 us
    pallas_call x1, Pallas kernels, body(): pl.pallas_call(functools.partial(contrast_kernel, 1.0 / math.sqrt(width))...  18.8 us
    pallas_call x1, Pallas kernels, body(): pl.pallas_call(functools.partial(last_backward, group, steps), grid_spec=...  17.5 us
    pallas_call x1, Pallas kernels, body(): pl.pallas_call(functools.partial(later_forward, group), grid_spec=pltpu.P...  13.2 us
  transfers between devices with their start and end apart: 4, of which 0 were waited for; matrix products, arithmetic and copies ran while one was open for 3% of the time, Pallas kernels for 0%

profile of v2, /device:TPU:0, one launch (start us, length us, event | category | flops | bytes accessed | tf_op | source)
XLA Modules:
  0.0 287.3 jit_solution(8889530313974419992)
XLA Ops:
  0.6 0.7 convert_element_type.14
  1.4 0.1 pad.11.clone
  1.5 1.0 maximum_maximum_fusion
  2.5 3.1 %collective-permute-start = (bf16[16,4096]{1,0:T(8,128)(2,1)S(1)}, bf16[16,4096]{1,0:T(8,128)(2,1)S(1)}, u32[]{:S(2)}, u32[]{:S(2)}) collective-permute-start(bf16[16,4096]{1,0:T(8,128)(2,1)S(1)} %maximum_maximum_fusion), channel_id=1, source_target_pairs={{0,2},{1,3},{2,0},{3,1},{4,6},{5,7},{6,4},{7,5},{8,10},{9,11},{10,... | collective-permute-start | bytes 393224 | tf_op jit(solution)/shard_map/ppermute | solution.py:38
  5.5 3.5 %collective-permute-start.1 = (bf16[16,4096]{1,0:T(8,128)(2,1)S(1)}, bf16[16,4096]{1,0:T(8,128)(2,1)S(1)}, u32[]{:S(2)}, u32[]{:S(2)}) collective-permute-start(bf16[16,4096]{1,0:T(8,128)(2,1)S(1)} %maximum_maximum_fusion), channel_id=1, source_target_pairs={{0,14},{1,15},{2,4},{3,5},{4,2},{5,3},{6,8},{7,9},{8,6},{9,7},{10,... | collective-permute-start | bytes 393224 | tf_op jit(solution)/shard_map/ppermute | solution.py:38
  9.1 0.0 collective-permute-start.2
  9.1 1.3 collective-permute-start.3
  10.4 0.1 pad.4.clone
  10.4 1.4 slice_bitcast_fusion.2
  11.8 1.5 slice_bitcast_fusion
  13.3 0.7 fusion.1
  14.0 1.3 fusion.2
  15.3 0.8 pad_maximum_fusion.1.wcat_ref
  16.1 0.0 copy-start.1
  16.1 0.1 copy.28
  16.2 0.7 reshape.54.index_ref
  16.8 0.7 copy.29
  17.6 0.0 collective-permute-done
  17.6 1.0 constant_dynamic-update-slice_fusion.3
  18.6 0.0 collective-permute-done.1
  18.6 0.0 collective-permute-done.2
  18.6 0.0 collective-permute-done.3
  18.7 0.3 slice_reduce_fusion
  18.9 0.2 compare_convert_fusion
  19.1 1.3 pad_maximum_fusion.feats_ref
  20.5 0.0 copy-done.1
  20.5 20.0 %first_forward.1 = (bf16[4096,128]{1,0:T(8,128)(2,1)}, bf16[4096,128]{1,0:T(8,128)(2,1)}, bf16[4096,128]{1,0:T(8,128)(2,1)}, bf16[4096,128]{1,0:T(8,128)(2,1)}) custom-call(s32[256]{0:T(256)} %reshape.54.index_ref, bf16[32,8,128,128]{3,2,1,0:T(8,128)(2,1)} %tiles_ref.7, bf16[32,20480]{1,0:T(8,128)(2,1)} %pad_maximum_fusion.feats_ref, ...), custom_call_target="tpu_custom_call" | custom-call | tf_op jit(solution)/shard_map/first_forward/pallas_call | solution.py:763
  40.5 32.7 %exchange.2 = (bf16[4096,128]{1,0:T(8,128)(2,1)}, bf16[4096,128]{1,0:T(8,128)(2,1)}, bf16[4096,128]{1,0:T(8,128)(2,1)}, bf16[4096,128]{1,0:T(8,128)(2,1)}) custom-call(bf16[4096,128]{1,0:T(8,128)(2,1)} %get-tuple-element.44.own.own_ref.before_ref), custom_call_target="tpu_custom_call" | custom-call | tf_op jit(solution)/shard_map/exchange/pallas_call | solution.py:143
  73.2 13.2 %later_forward.1 = (bf16[4096,128]{1,0:T(8,128)(2,1)}, bf16[4096,128]{1,0:T(8,128)(2,1)}, bf16[4096,128]{1,0:T(8,128)(2,1)}) custom-call(s32[256]{0:T(256)} %reshape.54.index_ref, bf16[32,8,128,128]{3,2,1,0:T(8,128)(2,1)} %tiles_ref.7, bf16[4096,128]{1,0:T(8,128)(2,1)} %get-tuple-element.45.below_ref, ...), custom_call_target="tpu_custom_call" | custom-call | tf_op jit(solution)/shard_map/later_forward/pallas_call | solution.py:779
  86.4 33.1 %exchange.3 = (bf16[4096,128]{1,0:T(8,128)(2,1)}, bf16[4096,128]{1,0:T(8,128)(2,1)}, bf16[4096,128]{1,0:T(8,128)(2,1)}, bf16[4096,128]{1,0:T(8,128)(2,1)}) custom-call(bf16[4096,128]{1,0:T(8,128)(2,1)} %get-tuple-element.49.own.own_ref), custom_call_target="tpu_custom_call" | custom-call | tf_op jit(solution)/shard_map/exchange/pallas_call | solution.py:143
  119.5 18.8 %contrast.1 = (f32[8,128]{1,0:T(8,128)}, f32[4096,128]{1,0:T(8,128)}, f32[4096,128]{1,0:T(8,128)}, f32[4096,128]{1,0:T(8,128)}, bf16[4096,128]{1,0:T(8,128)(2,1)}, /*index=5*/bf16[4096,128]{1,0:T(8,128)(2,1)}) custom-call(s32[1024]{0:T(1024)} %anchor_ref.1, s32[1024]{0:T(1024)} %get-tuple-element.91.positive_ref, s32[1024]{0:T(1024)} %get-tuple-element.92.negative_ref, ...), custom_call_target="tpu_custom_call" | custom-call | tf_op jit(solution)/shard_map/contrast/pallas_call | solution.py:801
  138.4 36.2 %give_back.2 = (bf16[4096,128]{1,0:T(8,128)(2,1)}, bf16[4096,128]{1,0:T(8,128)(2,1)}) custom-call(f32[4096,128]{1,0:T(8,128)} %get-tuple-element.55.direct_ref, f32[4096,128]{1,0:T(8,128)} %get-tuple-element.56.relay_ref, bf16[4096,128]{1,0:T(8,128)(2,1)} %get-tuple-element.57.sib_ref, bf16[4096,128]{1,0:T(8,128)(2,1)} %get-tuple-element.58.cross_ref), custom_call_target="tpu_custom_call" | custom-call | tf_op jit(solution)/shard_map/give_back/pallas_call | solution.py:216
  174.6 17.5 %last_backward.1 = (f32[128,128]{1,0:T(8,128)}, f32[128,128]{1,0:T(8,128)}, f32[128,128]{1,0:T(8,128)}, f32[4096,128]{1,0:T(8,128)}, f32[32,128,128]{2,1,0:T(8,1...) custom-call(s32[256]{0:T(256)} %reshape.54.index_ref, ...), custom_call_target="tpu_custom_call" | custom-call | tf_op jit(solution)/shard_map/last_backward/pallas_call | solution.py:829
  192.0 37.0 %give_back.3 = (bf16[4096,128]{1,0:T(8,128)(2,1)}, bf16[4096,128]{1,0:T(8,128)(2,1)}) custom-call(f32[4096,128]{1,0:T(8,128)} %bitcast.24, f32[4096,128]{1,0:T(8,128)} %bitcast.25, bf16[4096,128]{1,0:T(8,128)(2,1)} %bitcast.29, bf16[4096,128]{1,0:T(8,128)(2,1)} %bitcast.30), custom_call_target="tpu_custom_call" | custom-call | tf_op jit(solution)/shard_map/give_back/pallas_call | solution.py:216
  229.0 0.0 copy-start.4
  229.1 0.0 copy-start.3
  229.1 0.0 copy-start.2
  229.1 0.0 copy-start.5
  229.1 27.8 %first_backward.1 = (f32[128,128]{1,0:T(8,128)}, f32[128,128]{1,0:T(8,128)}, f32[128,128]{1,0:T(8,128)}, f32[32,128]{1,0:T(8,128)}) custom-call(s32[256]{0:T(256)} %reshape.54.index_ref, bf16[32,8,128,128]{3,2,1,0:T(8,128)(2,1)} %tiles_ref.7, f32[4096,128]{1,0:T(8,128)} %get-tuple-element.63.direct_ref, f32[32,128,128]{2,1,0:T(8,128)} %get-tuple-element.64.own_ref, ...), custom_call_target="tpu_custom_call" | custom-call | tf_op jit(solution)/shard_map/first_backward/pallas_call | solution.py:847
  256.9 0.8 constant_dynamic-update-slice_fusion.13
  257.8 0.0 copy-done.4
  257.8 0.8 constant_dynamic-update-slice_fusion.11
  258.6 0.0 copy-done.3
  258.7 0.8 constant_dynamic-update-slice_fusion.9
  259.5 0.0 copy-done.2
  259.5 0.7 constant_dynamic-update-slice_fusion.7
  260.2 0.0 copy-done.5
  260.3 0.0 copy-start
  260.3 0.8 copy-done
  261.0 18.9 %sum_all.1 = f32[896,128]{1,0:T(8,128)} custom-call(f32[896,128]{1,0:T(8,128)} %copy-done), custom_call_target="tpu_custom_call" | custom-call | tf_op jit(solution)/shard_map/sum_all/pallas_call | solution.py:294
  280.0 1.8 fusion.7
  281.7 1.3 slice.57
  283.0 1.3 slice.58
  284.3 1.2 slice.56
  (13 shorter events, 0.1 us)
Async XLA Ops:
  2.5 15.1 %collective-permute-start = (bf16[16,4096]{1,0:T(8,128)(2,1)S(1)}, bf16[16,4096]{1,0:T(8,128)(2,1)S(1)}, u32[]{:S(2)}, u32[]{:S(2)}) collective-permute-start(bf16[16,4096]{1,0:T(8,128)(2,1)S(1)} %maximum_maximum_fusion), channel_id=1, source_target_pairs={{0,2},{1,3},{2,0},{3,1},{4,6},{5,7},{6,4},{7,5},{8,10},{9,11},{10,... | collective-permute-start | bytes 393224 | tf_op jit(solution)/shard_map/ppermute | solution.py:38
  5.5 13.1 %collective-permute-start.1 = (bf16[16,4096]{1,0:T(8,128)(2,1)S(1)}, bf16[16,4096]{1,0:T(8,128)(2,1)S(1)}, u32[]{:S(2)}, u32[]{:S(2)}) collective-permute-start(bf16[16,4096]{1,0:T(8,128)(2,1)S(1)} %maximum_maximum_fusion), channel_id=1, source_target_pairs={{0,14},{1,15},{2,4},{3,5},{4,2},{5,3},{6,8},{7,9},{8,6},{9,7},{10,... | collective-permute-start | bytes 393224 | tf_op jit(solution)/shard_map/ppermute | solution.py:38
  9.1 9.5 %collective-permute-start.2 = (bf16[16,4096]{1,0:T(8,128)(2,1)S(1)}, bf16[16,4096]{1,0:T(8,128)(2,1)S(1)}, u32[]{:S(2)}, u32[]{:S(2)}) collective-permute-start(bf16[16,4096]{1,0:T(8,128)(2,1)S(1)} %maximum_maximum_fusion), channel_id=1, source_target_pairs={{0,1},{1,0},{2,3},{3,2},{4,5},{5,4},{6,7},{7,6},{8,9},{9,8},{10,11... | collective-permute-start | bytes 393224 | tf_op jit(solution)/shard_map/ppermute | solution.py:38
  9.1 9.6 %collective-permute-start.3 = (bf16[16,4096]{1,0:T(8,128)(2,1)S(1)}, bf16[16,4096]{1,0:T(8,128)(2,1)S(1)}, u32[]{:S(2)}, u32[]{:S(2)}) collective-permute-start(bf16[16,4096]{1,0:T(8,128)(2,1)S(1)} %maximum_maximum_fusion), channel_id=1, source_target_pairs={{0,15},{1,2},{2,1},{3,4},{4,3},{5,6},{6,5},{7,8},{8,7},{9,10},{10,... | collective-permute-start | bytes 393224 | tf_op jit(solution)/shard_map/ppermute | solution.py:38
  16.1 4.4 %copy-start.1 = (bf16[32,128]{1,0:T(8,128)(2,1)}, bf16[32,128]{1,0:T(8,128)(2,1)S(1)}, u32[]{:S(2)}) copy-start(bf16[32,128]{1,0:T(8,128)(2,1)S(1)} %pad_maximum_fusion.1.wcat_ref) | copy-start | bytes 24580
  229.0 28.7 %copy-start.4 = (f32[128,128]{1,0:T(8,128)S(1)}, f32[128,128]{1,0:T(8,128)}, u32[]{:S(2)}) copy-start(f32[128,128]{1,0:T(8,128)} %get-tuple-element.75) | copy-start | bytes 196612
  229.1 29.6 %copy-start.3 = (f32[128,128]{1,0:T(8,128)S(1)}, f32[128,128]{1,0:T(8,128)}, u32[]{:S(2)}) copy-start(f32[128,128]{1,0:T(8,128)} %get-tuple-element.77) | copy-start | bytes 196612
  229.1 30.4 %copy-start.2 = (f32[128,128]{1,0:T(8,128)S(1)}, f32[128,128]{1,0:T(8,128)}, u32[]{:S(2)}) copy-start(f32[128,128]{1,0:T(8,128)} %get-tuple-element.79) | copy-start | bytes 196612
  229.1 31.2 %copy-start.5 = (f32[8,128]{1,0:T(8,128)S(1)}, f32[8,128]{1,0:T(8,128)}, u32[]{:S(2)}) copy-start(f32[8,128]{1,0:T(8,128)} %get-tuple-element.81) | copy-start | bytes 12292
  260.3 0.8 copy-start

commit v3 on v2

--- a/solution.py
+++ b/solution.py
@@ -30,28 +30,7 @@
     )
 
 
-CHUNKS = 8
-
-
-def permute(value, target_of):
-    count = lax.axis_size("phi")
-    return lax.ppermute(value, "phi", [(s, target_of(s) % count) for s in range(count)])
-
-
-def direct_target(s):
-    return s ^ 2
-
-
-def relayed_target(s):
-    return s + 2 if (s // 2) % 2 else s - 2
-
-
-def sibling_target(s):
-    return s ^ 1
-
-
-def cross_target(s):
-    return s + 1 if s % 2 else s - 1
+CHUNKS = 16
 
 
 def peers():
@@ -135,6 +114,49 @@
         first[i].wait_send()
         second[i].wait_send()
         cross_a[i].wait()
+
+
+def feature_kernel(own_ref, out_ref, sends, recvs):
+    count = lax.axis_size("phi")
+    me = lax.axis_index("phi")
+    odd_pair = (me // 2) % 2
+    odd_core = me % 2
+    far = (me - 2 + 4 * odd_pair + count) % count
+    cross = (me - 1 + 2 * odd_core + count) % count
+    direct = me + 2 - 4 * odd_pair
+    sibling = me + 1 - 2 * odd_core
+    hits = own_ref.shape[1]
+    targets = (direct, far, sibling, cross)
+    greet(targets)
+    copies = [
+        remote(
+            own_ref,
+            out_ref.at[:, pl.ds(place * hits, hits)],
+            sends.at[k],
+            recvs.at[k],
+            targets[k],
+        )
+        for k, place in enumerate((0, 2, 3, 4))
+    ]
+    for copy in copies:
+        copy.start()
+    out_ref[:, pl.ds(hits, hits)] = own_ref[...]
+    for copy in copies:
+        copy.wait()
+
+
+def feature_window(packed):
+    depth, hits = packed.shape
+    vmem = pl.BlockSpec(memory_space=pltpu.VMEM)
+    return pl.pallas_call(
+        feature_kernel,
+        in_specs=[vmem],
+        out_specs=vmem,
+        out_shape=jax.ShapeDtypeStruct((depth, 5 * hits), BF16),
+        scratch_shapes=[pltpu.SemaphoreType.DMA((4,))] * 2,
+        compiler_params=pltpu.CompilerParams(collective_id=4, has_side_effects=True),
+        name="features",
+    )(packed)
 
 
 def window_pieces(latents):
@@ -230,8 +252,16 @@
 
 
 def sum_kernel(
-    pairs, x_ref, out_ref, half_in, acc_ref, slots_in, all_ref, s0, r0, s1, r1, s2, r2, s3, r3
+    pairs, parts, *refs
 ):
+    part_refs = refs[:parts]
+    out_ref, x_ref, half_in, acc_ref, slots_in, all_ref, s0, r0, s1, r1, s2, r2, s3, r3 = refs[parts:]
+    at = 0
+    for part_ref in part_refs:
+        x_ref[pl.ds(at, part_ref.shape[0]), :] = part_ref[...]
+        at += part_ref.shape[0]
+    if at < x_ref.shape[0]:
+        x_ref[pl.ds(at, x_ref.shape[0] - at), :] = jnp.zeros((x_ref.shape[0] - at, x_ref.shape[1]), F32)
     me = lax.axis_index("phi")
     pair, core = me // 2, me % 2
     sibling = me + 1 - 2 * core
@@ -282,21 +312,21 @@
     out_ref[...] = all_ref[...]
 
 
-def sum_all(value):
+def sum_all(values):
     pairs = lax.axis_size("phi") // 2
-    rows, width = value.shape
+    rows, width = sum(value.shape[0] for value in values), values[0].shape[1]
     chunk = -(-rows // (16 * pairs)) * 8
     total = 2 * pairs * chunk
-    value = jnp.concatenate([value, jnp.zeros((total - rows, width), F32)], axis=0)
     vmem = pl.BlockSpec(memory_space=pltpu.VMEM)
     one = pltpu.SemaphoreType.DMA((1,))
     many = pltpu.SemaphoreType.DMA((pairs - 1,))
     return pl.pallas_call(
-        functools.partial(sum_kernel, pairs),
-        in_specs=[vmem],
+        functools.partial(sum_kernel, pairs, len(values)),
+        in_specs=[vmem] * len(values),
         out_specs=vmem,
         out_shape=jax.ShapeDtypeStruct((total, width), F32),
         scratch_shapes=[
+            pltpu.VMEM((total, width), F32),
             pltpu.VMEM((total // 2, width), F32),
             pltpu.VMEM((total // 2, width), F32),
             pltpu.VMEM((pairs - 1, chunk, width), F32),
@@ -307,7 +337,7 @@
             collective_id=3, has_side_effects=True, vmem_limit_bytes=VMEM_BYTES
         ),
         name="sum_all",
-    )(value)
+    )(*values)
 
 
 def aggregate_group(index_ref, tiles_ref, window_ref, step, group, slots, rows):
@@ -732,16 +762,7 @@
     packed = jnp.concatenate(
         [hit_feats, layer_ids.astype(BF16)[None, :], jnp.zeros((pad, hits), BF16)], axis=0
     )
-    packed = jnp.concatenate(
-        [
-            permute(packed, direct_target),
-            packed,
-            permute(packed, relayed_target),
-            permute(packed, sibling_target),
-            permute(packed, cross_target),
-        ],
-        axis=1,
-    )
+    packed = feature_window(packed)
     feature_pad = -features % 16
     onehot = (
         jnp.arange(kinds, dtype=jnp.int32)[:, None].astype(BF16) == packed[features][None, :]
@@ -864,9 +885,7 @@
         index, edge_tiles, direct, own, total, sib, hidden, before, aggregated,
         w_self[0], w_agg[0], w_out[0], feats, wcat, wcat.T,
     )
-    late = sum_all(
-        jnp.concatenate([gout0, gout1, gself0, gself1, gagg0, gagg1, genc, loss_part], axis=0)
-    )
+    late = sum_all([gout0, gout1, gself0, gself1, gagg0, gagg1, genc, loss_part])
 
     triplet_total = triplets * lax.axis_size("phi")
     base = 6 * width

time: 289 us -> 289 us (level)
  Pallas kernels: 255 us -> 268 us
  starting transfers between devices: 7.9 us -> 0 us
  local copies, waits for them, and re-layouts: 14.4 us -> 9.78 us
    pallas_call x1 -> x2, Pallas kernels: 18.9 us -> 34.3 us  [the longest x1 19.9 us: sum_all(): pl.pallas_call(functools.partial(sum_kernel, pairs, len(values)), in_spec...]
    ppermute x4 -> x0, starting transfers between devices: 7.9 us -> none  [permute(): lax.ppermute(value, 'phi', [(s, target_of(s) % count) for s in range(coun...]
    unnamed x23 -> x16, local copies, waits for them, and re-layouts: 4.1 us -> 0.04 us
  transfers between devices with their start and end apart: 4 -> 0, of which waited for: 0 -> 0; matrix products, arithmetic and copies ran while one was open for 3% -> 0% of each run, Pallas kernels for 0% -> 0%
where the time goes in v3:
time: 289 us; the launch traced here: 288 us
  Pallas kernels  268 us (93%)
  local copies, waits for them, and re-layouts  9.78 us (3%)
  other arithmetic  7.02 us (2%)
    pallas_call x2, Pallas kernels, return_pieces(): pl.pallas_call(return_kernel, in_specs=[vmem] * 4, out_specs=[vmem] * 2,...  71.8 us
    pallas_call x2, Pallas kernels, window_pieces(): pl.pallas_call(exchange_kernel, in_specs=[any_spec], out_specs=[any_spec]...  65.1 us
    pallas_call x1, Pallas kernels, body(): pl.pallas_call(functools.partial(first_backward, group, steps), grid_spec...  27.6 us
    pallas_call x1, Pallas kernels, body(): pl.pallas_call(functools.partial(first_forward, group), grid_spec=pltpu.P...  20 us
    pallas_call x1, Pallas kernels, sum_all(): pl.pallas_call(functools.partial(sum_kernel, pairs, len(values)), in_spec...  19.9 us
    pallas_call x1, Pallas kernels, body(): pl.pallas_call(functools.partial(contrast_kernel, 1.0 / math.sqrt(width))...  18.8 us
    pallas_call x1, Pallas kernels, body(): pl.pallas_call(functools.partial(last_backward, group, steps), grid_spec=...  17.5 us
    pallas_call x1, Pallas kernels, feature_window(): pl.pallas_call(feature_kernel, in_specs=[vmem], out_specs=vmem, out_shape...  14.4 us

profile of v3, /device:TPU:0, one launch (start us, length us, event | category | flops | bytes accessed | tf_op | source)
XLA Modules:
  0.0 287.9 jit_solution(17510286654980324065)
XLA Ops:
  0.7 0.7 fusion.1
  1.4 0.1 copy.28
  1.5 0.7 reshape.54.index_ref
  2.1 0.7 convert_element_type.14
  2.9 0.1 pad.8.clone
  3.0 1.6 maximum_maximum_fusion.own_ref
  4.6 0.0 copy-start.2
  4.6 0.0 copy-start.3
  4.6 0.0 copy-start.4
  4.6 0.0 copy-start.5
  4.6 0.0 copy-start.1
  4.6 14.4 %features.1 = bf16[16,20480]{1,0:T(8,128)(2,1)} custom-call(bf16[16,4096]{1,0:T(8,128)(2,1)} %maximum_maximum_fusion.own_ref), custom_call_target="tpu_custom_call" | custom-call | tf_op jit(solution)/shard_map/features/pallas_call | solution.py:151
  19.1 1.2 slice_reduce_fusion
  20.3 0.2 compare_convert_fusion
  20.6 0.1 pad.4.clone
  20.6 2.4 pad_maximum_fusion.feats_ref
  23.1 0.0 copy-done.2
  23.1 0.0 copy-done.3
  23.1 0.7 slice_bitcast_fusion
  23.7 0.0 copy-done.4
  23.7 0.0 copy-done.5
  23.7 0.7 pad_maximum_fusion.1.wcat_ref
  24.4 0.0 copy-done.1
  24.4 0.6 slice_bitcast_fusion.2
  25.0 20.0 %first_forward.1 = (bf16[4096,128]{1,0:T(8,128)(2,1)}, bf16[4096,128]{1,0:T(8,128)(2,1)}, bf16[4096,128]{1,0:T(8,128)(2,1)}, bf16[4096,128]{1,0:T(8,128)(2,1)}) custom-call(s32[256]{0:T(256)} %reshape.54.index_ref, bf16[32,8,128,128]{3,2,1,0:T(8,128)(2,1)} %tiles_ref.7, bf16[32,20480]{1,0:T(8,128)(2,1)} %pad_maximum_fusion.feats_ref, ...), custom_call_target="tpu_custom_call" | custom-call | tf_op jit(solution)/shard_map/first_forward/pallas_call | solution.py:784
  45.1 33.4 %exchange.2 = (bf16[4096,128]{1,0:T(8,128)(2,1)}, bf16[4096,128]{1,0:T(8,128)(2,1)}, bf16[4096,128]{1,0:T(8,128)(2,1)}, bf16[4096,128]{1,0:T(8,128)(2,1)}) custom-call(bf16[4096,128]{1,0:T(8,128)(2,1)} %get-tuple-element.44.own.own_ref.before_ref), custom_call_target="tpu_custom_call" | custom-call | tf_op jit(solution)/shard_map/exchange/pallas_call | solution.py:165
  78.4 0.0 copy-start.6
  78.4 0.0 copy-start.7
  78.5 13.3 %later_forward.1 = (bf16[4096,128]{1,0:T(8,128)(2,1)}, bf16[4096,128]{1,0:T(8,128)(2,1)}, bf16[4096,128]{1,0:T(8,128)(2,1)}) custom-call(s32[256]{0:T(256)} %reshape.54.index_ref, bf16[32,8,128,128]{3,2,1,0:T(8,128)(2,1)} %tiles_ref.7, bf16[4096,128]{1,0:T(8,128)(2,1)} %get-tuple-element.45.below_ref, ...), custom_call_target="tpu_custom_call" | custom-call | tf_op jit(solution)/shard_map/later_forward/pallas_call | solution.py:800
  91.8 31.7 %exchange.3 = (bf16[4096,128]{1,0:T(8,128)(2,1)}, bf16[4096,128]{1,0:T(8,128)(2,1)}, bf16[4096,128]{1,0:T(8,128)(2,1)}, bf16[4096,128]{1,0:T(8,128)(2,1)}) custom-call(bf16[4096,128]{1,0:T(8,128)(2,1)} %get-tuple-element.49.own.own_ref), custom_call_target="tpu_custom_call" | custom-call | tf_op jit(solution)/shard_map/exchange/pallas_call | solution.py:165
  123.5 0.0 copy-done.6
  123.5 0.0 copy-done.7
  123.5 0.6 fusion.2
  124.2 18.8 %contrast.1 = (f32[8,128]{1,0:T(8,128)}, f32[4096,128]{1,0:T(8,128)}, f32[4096,128]{1,0:T(8,128)}, f32[4096,128]{1,0:T(8,128)}, bf16[4096,128]{1,0:T(8,128)(2,1)}, /*index=5*/bf16[4096,128]{1,0:T(8,128)(2,1)}) custom-call(s32[1024]{0:T(1024)} %anchor_ref.1, s32[1024]{0:T(1024)} %get-tuple-element.91.positive_ref, s32[1024]{0:T(1024)} %get-tuple-element.92.negative_ref, ...), custom_call_target="tpu_custom_call" | custom-call | tf_op jit(solution)/shard_map/contrast/pallas_call | solution.py:822
  143.0 36.7 %give_back.2 = (bf16[4096,128]{1,0:T(8,128)(2,1)}, bf16[4096,128]{1,0:T(8,128)(2,1)}) custom-call(f32[4096,128]{1,0:T(8,128)} %get-tuple-element.55.direct_ref, f32[4096,128]{1,0:T(8,128)} %get-tuple-element.56.relay_ref, bf16[4096,128]{1,0:T(8,128)(2,1)} %get-tuple-element.57.sib_ref, bf16[4096,128]{1,0:T(8,128)(2,1)} %get-tuple-element.58.cross_ref), custom_call_target="tpu_custom_call" | custom-call | tf_op jit(solution)/shard_map/give_back/pallas_call | solution.py:238
  179.7 17.5 %last_backward.1 = (f32[128,128]{1,0:T(8,128)}, f32[128,128]{1,0:T(8,128)}, f32[128,128]{1,0:T(8,128)}, f32[4096,128]{1,0:T(8,128)}, f32[32,128,128]{2,1,0:T(8,1...) custom-call(s32[256]{0:T(256)} %reshape.54.index_ref, ...), custom_call_target="tpu_custom_call" | custom-call | tf_op jit(solution)/shard_map/last_backward/pallas_call | solution.py:850
  197.2 0.0 copy-start
  197.2 35.1 %give_back.3 = (bf16[4096,128]{1,0:T(8,128)(2,1)}, bf16[4096,128]{1,0:T(8,128)(2,1)}) custom-call(f32[4096,128]{1,0:T(8,128)} %bitcast.25, f32[4096,128]{1,0:T(8,128)} %bitcast.26, bf16[4096,128]{1,0:T(8,128)(2,1)} %bitcast.29, bf16[4096,128]{1,0:T(8,128)(2,1)} %bitcast.30), custom_call_target="tpu_custom_call" | custom-call | tf_op jit(solution)/shard_map/give_back/pallas_call | solution.py:238
  232.3 0.0 copy-done
  232.3 0.7 copy.29
  233.0 27.6 %first_backward.1 = (f32[128,128]{1,0:T(8,128)}, f32[128,128]{1,0:T(8,128)}, f32[128,128]{1,0:T(8,128)}, f32[32,128]{1,0:T(8,128)}) custom-call(s32[256]{0:T(256)} %reshape.54.index_ref, bf16[32,8,128,128]{3,2,1,0:T(8,128)(2,1)} %tiles_ref.7, f32[4096,128]{1,0:T(8,128)} %get-tuple-element.63.direct_ref, f32[32,128,128]{2,1,0:T(8,128)} %get-tuple-element.64.own_ref, ...), custom_call_target="tpu_custom_call" | custom-call | tf_op jit(solution)/shard_map/first_backward/pallas_call | solution.py:868
  260.7 19.9 %sum_all.1 = f32[896,128]{1,0:T(8,128)} custom-call(f32[128,128]{1,0:T(8,128)} %get-tuple-element.74.refs_0_, f32[128,128]{1,0:T(8,128)} %get-tuple-element.75.refs_1_, f32[128,128]{1,0:T(8,128)} %get-tuple-element.76.refs_2_, f32[128,128]{1,0:T(8,128)} %get-tuple-element.77.refs_3_, f32[128,128]{1,0:T(8,128)} %get-tuple-element.78.refs_4_, ...), custom_call_target="tpu_custom_call" | custom-call | tf_op jit(solution)/shard_map/sum_all/pallas_call | solution.py:323
  280.5 1.8 fusion.7
  282.3 1.3 slice.57
  283.6 1.3 slice.58
  284.9 1.2 slice.56
  (4 shorter events, 0.0 us)
Async XLA Ops:
  4.6 18.4 %copy-start.2 = (bf16[2,128,128]{2,1,0:T(8,128)(2,1)S(1)}, bf16[2,128,128]{2,1,0:T(8,128)(2,1)}, u32[]{:S(2)}) copy-start(bf16[2,128,128]{2,1,0:T(8,128)(2,1)} %param.25) | copy-start | bytes 196612
  4.6 18.5 %copy-start.3 = (bf16[2,128,128]{2,1,0:T(8,128)(2,1)S(1)}, bf16[2,128,128]{2,1,0:T(8,128)(2,1)}, u32[]{:S(2)}) copy-start(bf16[2,128,128]{2,1,0:T(8,128)(2,1)} %param.24) | copy-start | bytes 196612
  4.6 19.1 %copy-start.4 = (bf16[16,128]{1,0:T(8,128)(2,1)S(1)}, bf16[16,128]{1,0:T(8,128)(2,1)}, u32[]{:S(2)}) copy-start(bf16[16,128]{1,0:T(8,128)(2,1)} %param.22) | copy-start | bytes 12292
  4.6 19.1 %copy-start.5 = (bf16[12,128]{1,0:T(8,128)(2,1)S(1)}, bf16[12,128]{1,0:T(8,128)(2,1)}, u32[]{:S(2)}) copy-start(bf16[12,128]{1,0:T(8,128)(2,1)} %param.21) | copy-start | bytes 9220
  4.6 19.8 %copy-start.1 = (bf16[2,128,128]{2,1,0:T(8,128)(2,1)S(1)}, bf16[2,128,128]{2,1,0:T(8,128)(2,1)}, u32[]{:S(2)}) copy-start(bf16[2,128,128]{2,1,0:T(8,128)(2,1)} %param.23) | copy-start | bytes 196612
  78.4 45.1 %copy-start.6 = (s32[1024]{0:T(1024)S(1)}, s32[1024]{0:T(1024)}, u32[]{:S(2)}) copy-start(s32[1024]{0:T(1024)} %param.19) | copy-start | bytes 12292
  78.4 45.1 %copy-start.7 = (s32[1024]{0:T(1024)S(1)}, s32[1024]{0:T(1024)}, u32[]{:S(2)}) copy-start(s32[1024]{0:T(1024)} %param.20) | copy-start | bytes 12292
  197.2 35.1 %copy-start = (bf16[32,128]{1,0:T(8,128)(2,1)S(1)}, bf16[32,128]{1,0:T(8,128)(2,1)}, u32[]{:S(2)}) copy-start(bf16[32,128]{1,0:T(8,128)(2,1)} %pad_maximum_fusion.1.wcat_ref) | copy-start | bytes 24580
